TPU v7x, 32 devices: a whole 2x2x4 slice. The times are simulated.
32 devices in a mesh: row: 8 (over z, x), col: 4 (over y, core).
Axes of the slice: x: 2, y: 2, z: 4, core: 2. Of those that a mesh axis runs over, the one named last changes fastest.
Arguments:
- layer_input: bfloat16 [16384, 960], P(('row', 'col')), may hold values from -6 to 6
- norm1_gain: float32 [960], replicated, may hold values from 0.5 to 1.5
- w_qkv: bfloat16 [960, 1600], P('row', 'col'), may hold values from -0.1875 to 0.1875
- w_out: bfloat16 [960, 960], P('row', 'col'), may hold values from -1.5 to 1.5
- norm2_gain: float32 [960], replicated, may hold values from 0.5 to 1.5
- w_gate: bfloat16 [960, 2560], P('row', 'col'), may hold values from -0.1875 to 0.1875
- w_up: bfloat16 [960, 2560], P('row', 'col'), may hold values from -0.1875 to 0.1875
- w_down: bfloat16 [960, 2560], P('row', 'col'), may hold values from -0.15625 to 0.15625
- out_cotangent: bfloat16 [16384, 960], P(('row', 'col')), may hold values from -6 to 6
- seq_lengths: int32 [8, 3], P('row'), may hold values from 1 to 1024, 2048 in all within a row
- position_ids: int32 [16384], P(('row', 'col')), may hold values from 0 to 4094, as said below
- deal_rows: int32 [32, 8], P(('row', 'col')), may hold values from 0 to 7, each once within a row
Outputs:
- layer_output: bfloat16 [16384, 960], P(('row', 'col'))
- grad_input: bfloat16 [16384, 960], P(('row', 'col'))
- grad_norm1: float32 [960], replicated
- grad_qkv: float32 [960, 1600], P('row', 'col')
- grad_out: float32 [960, 960], P('row', 'col')
- grad_norm2: float32 [960], replicated
- grad_gate: float32 [960, 2560], P('row', 'col')
- grad_up: float32 [960, 2560], P('row', 'col')
- grad_down: float32 [960, 2560], P('row', 'col')
Inputs may be any that keep to these rules, and one draw needn't show every extreme that they name: Each row of seq_lengths gives the lengths of the 3 sequences packed in order into one row group of 2048 dealt rows; each row sums to 2048, and its largest entry is exactly 1024. `position_ids`: within each aligned group of 2048 dealt rows the ids start at 0 and rise by 1 or 2 from one row to the next; in some group they rise by 2 at every row. `deal_rows`: each row is a permutation of the 8 row groups.
All inputs are finite; a program needn't handle non-finite values.
Results may differ from a plain program's by a relative error of at most 0.015.
Values may be sent and summed in bfloat16 or wider, within the bound.
A program may use at most 128 MiB of HBM per device.

v0:
```python
import math

import jax
import jax.numpy as jnp
from jax import lax
from jax.sharding import PartitionSpec as P

QUERY_HEADS = 15
KEY_VALUE_HEADS = 5
HEAD_DIMENSION = 64
QUERY_FEATURES = 960
KEY_FEATURES = 320


EPS = 1e-05
NEG_FILL = -1e30
THETA = 10000.0


def matmul(left_mat, right_mat):
    return jnp.dot(left_mat, right_mat, preferred_element_type=jnp.float32)


def matmul_nt(left_mat, right_mat):
    return lax.dot_general(
        left_mat, right_mat, (((1,), (1,)), ((), ())), preferred_element_type=jnp.float32
    )


def matmul_tn(left_mat, right_mat):
    return lax.dot_general(
        left_mat, right_mat, (((0,), (0,)), ((), ())), preferred_element_type=jnp.float32
    )


def rms_scale(values):
    return lax.rsqrt(jnp.mean(values * values, axis=1, keepdims=True) + EPS)


def rope_tables(position, head_size):
    half_size = head_size // 2
    inverse = jnp.exp(
        jnp.arange(half_size, dtype=jnp.float32) * (-2.0 * math.log(THETA) / head_size)
    )
    angles = position.astype(jnp.float32)[:, None] * inverse[None, :]
    return (jnp.cos(angles), jnp.sin(angles))


def apply_rotation(values, cosine_table, sine_table, head_count):
    pieces = values.reshape(values.shape[0], head_count, -1)
    half_size = pieces.shape[2] // 2
    first_half = pieces[:, :, :half_size]
    second_half = pieces[:, :, half_size:]
    cos_wide = cosine_table[:, None, :]
    sin_wide = sine_table[:, None, :]
    turned = jnp.concatenate(
        [
            first_half * cos_wide - second_half * sin_wide,
            second_half * cos_wide + first_half * sin_wide,
        ],
        axis=2,
    )
    return turned.reshape(values.shape)


def reverse_rotation(values, cosine_table, sine_table, head_count):
    pieces = values.reshape(values.shape[0], head_count, -1)
    half_size = pieces.shape[2] // 2
    first_half = pieces[:, :, :half_size]
    second_half = pieces[:, :, half_size:]
    cos_wide = cosine_table[:, None, :]
    sin_wide = sine_table[:, None, :]
    turned = jnp.concatenate(
        [
            first_half * cos_wide + second_half * sin_wide,
            second_half * cos_wide - first_half * sin_wide,
        ],
        axis=2,
    )
    return turned.reshape(values.shape)


def gather_rows(values):
    return lax.all_gather(values, "col", axis=0, tiled=True)


def regroup_tokens(values):
    return lax.all_to_all(values, "col", split_axis=0, concat_axis=1, tiled=True)


def regroup_columns(values):
    return lax.all_to_all(values, "col", split_axis=1, concat_axis=0, tiled=True)


def spread_sum(products, own_rows):
    result = jnp.zeros((lax.axis_size("col") * own_rows, products[0][1].shape[0]), jnp.float32)
    for left_mat, right_mat in products:
        result = result + matmul_nt(left_mat, right_mat)
    return lax.psum_scatter(result, "col", scatter_dimension=0, tiled=True)


def attend(query_heads, heads_of_key, heads_of_value, allowed, factor):
    heads_per_group = query_heads.shape[0] // heads_of_key.shape[0]

    def one_head(unused, element):
        query_rows, head_index = element
        key_rows = lax.dynamic_index_in_dim(
            heads_of_key, head_index // heads_per_group, 0, keepdims=False
        )
        value_rows = lax.dynamic_index_in_dim(
            heads_of_value, head_index // heads_per_group, 0, keepdims=False
        )
        scores = jnp.where(allowed, matmul_nt(query_rows, key_rows) * factor, NEG_FILL)
        row_max = jnp.max(scores, axis=1, keepdims=True)
        weights = jnp.exp(scores - row_max)
        row_total = jnp.sum(weights, axis=1, keepdims=True)
        prob_low = (weights / row_total).astype(jnp.bfloat16)
        logsum = row_max[:, 0] + jnp.log(row_total[:, 0])
        return (unused, (matmul(prob_low, value_rows), logsum))

    head_ids = jnp.arange(query_heads.shape[0], dtype=jnp.int32)
    ignored, (head_outputs, logsum) = lax.scan(
        one_head, jnp.zeros((), jnp.float32), (query_heads, head_ids)
    )
    return (head_outputs, logsum)


def attend_back(query_heads, heads_of_key, heads_of_value, grad_heads, logsum, allowed, factor):
    heads_per_group = query_heads.shape[0] // heads_of_key.shape[0]

    def one_head(state, element):
        key_acc, value_acc = state
        query_rows, grad_rows, head_sum, head_index = element
        kv_index = head_index // heads_per_group
        key_rows = lax.dynamic_index_in_dim(heads_of_key, kv_index, 0, keepdims=False)
        value_rows = lax.dynamic_index_in_dim(heads_of_value, kv_index, 0, keepdims=False)
        scores = jnp.where(allowed, matmul_nt(query_rows, key_rows) * factor, NEG_FILL)
        probs = jnp.exp(scores - head_sum[:, None])
        prob_grad = matmul_nt(grad_rows, value_rows)
        score_grad = (
            probs * (prob_grad - jnp.sum(probs * prob_grad, axis=1, keepdims=True))
        ).astype(jnp.bfloat16)
        query_grad = matmul(score_grad, key_rows) * factor
        key_grad = matmul_tn(score_grad, query_rows) * factor
        value_grad = matmul_tn(probs.astype(jnp.bfloat16), grad_rows)
        key_acc = lax.dynamic_update_index_in_dim(
            key_acc,
            lax.dynamic_index_in_dim(key_acc, kv_index, 0, keepdims=False) + key_grad,
            kv_index,
            0,
        )
        value_acc = lax.dynamic_update_index_in_dim(
            value_acc,
            lax.dynamic_index_in_dim(value_acc, kv_index, 0, keepdims=False) + value_grad,
            kv_index,
            0,
        )
        return ((key_acc, value_acc), query_grad)

    head_ids = jnp.arange(query_heads.shape[0], dtype=jnp.int32)
    empty = jnp.zeros(heads_of_key.shape, jnp.float32)
    (key_acc, value_acc), query_grads = lax.scan(
        one_head, (empty, empty), (query_heads, grad_heads, logsum, head_ids)
    )
    return (query_grads, key_acc, value_acc)


def on_device(
    layer_input,
    norm1_gain,
    w_qkv,
    w_out,
    norm2_gain,
    w_gate,
    w_up,
    w_down,
    out_cotangent,
    seq_lengths,
    position_ids,
    deal_rows,
):
    own_rows, model_width = layer_input.shape
    row_devices = lax.axis_size("row")
    col_devices = lax.axis_size("col")
    block_rows = own_rows // row_devices
    rows_per_group = own_rows * col_devices
    row_ids = jnp.arange(row_devices, dtype=jnp.int32)
    targets = deal_rows[0]
    sender = jnp.sum(jnp.where(targets[:, None] == row_ids[None, :], row_ids[:, None], 0), axis=0)
    input_blocks = jnp.take(
        layer_input.reshape(row_devices, block_rows, model_width), sender, axis=0
    ).reshape(own_rows, model_width)
    cot_blocks = jnp.take(
        out_cotangent.reshape(row_devices, block_rows, model_width), sender, axis=0
    ).reshape(own_rows, model_width)
    dealt_input, dealt_cot = (
        lax.all_to_all(input_blocks, "row", split_axis=0, concat_axis=0, tiled=True),
        lax.all_to_all(cot_blocks, "row", split_axis=0, concat_axis=0, tiled=True),
    )
    qkv_mat, out_mat, gate_mat, up_mat, down_mat = (
        lax.all_gather(w_qkv, "row", axis=0, tiled=True),
        lax.all_gather(w_out, "row", axis=0, tiled=True),
        lax.all_gather(w_gate, "row", axis=0, tiled=True),
        lax.all_gather(w_up, "row", axis=0, tiled=True),
        lax.all_gather(w_down, "row", axis=0, tiled=True),
    )
    inputs_f = dealt_input.astype(jnp.float32)
    scale_one = rms_scale(inputs_f)
    normed_one = inputs_f * scale_one
    xn_one = (normed_one * norm1_gain).astype(jnp.bfloat16)
    xn_one_rows = gather_rows(xn_one)
    query_key_value_local = regroup_tokens(matmul(xn_one_rows, qkv_mat).astype(jnp.bfloat16))
    factor = 1.0 / math.sqrt(HEAD_DIMENSION)
    cosine_table, sine_table = rope_tables(position_ids, HEAD_DIMENSION)
    query_r = apply_rotation(
        query_key_value_local[:, :QUERY_FEATURES].astype(jnp.float32),
        cosine_table,
        sine_table,
        QUERY_HEADS,
    ).astype(jnp.bfloat16)
    key_repeated = apply_rotation(
        query_key_value_local[:, QUERY_FEATURES : QUERY_FEATURES + KEY_FEATURES].astype(
            jnp.float32
        ),
        cosine_table,
        sine_table,
        KEY_VALUE_HEADS,
    ).astype(jnp.bfloat16)
    value_own = query_key_value_local[:, QUERY_FEATURES + KEY_FEATURES :]
    key_full, value_full = (
        lax.all_gather(key_repeated, "col", axis=0, tiled=True),
        lax.all_gather(value_own, "col", axis=0, tiled=True),
    )
    col_index = lax.axis_index("col")
    key_ids = jnp.arange(rows_per_group, dtype=jnp.int32)
    query_ids = col_index * own_rows + jnp.arange(own_rows, dtype=jnp.int32)
    bounds = jnp.cumsum(seq_lengths[0])
    key_seg = jnp.sum((key_ids[:, None] >= bounds[None, :]).astype(jnp.int32), axis=1)
    query_seg = jnp.sum((query_ids[:, None] >= bounds[None, :]).astype(jnp.int32), axis=1)
    allowed = (query_seg[:, None] == key_seg[None, :]) & (key_ids[None, :] <= query_ids[:, None])
    query_heads = query_r.reshape(own_rows, QUERY_HEADS, HEAD_DIMENSION).transpose(1, 0, 2)
    heads_of_key = key_full.reshape(rows_per_group, KEY_VALUE_HEADS, HEAD_DIMENSION).transpose(
        1, 0, 2
    )
    heads_of_value = value_full.reshape(rows_per_group, KEY_VALUE_HEADS, HEAD_DIMENSION).transpose(
        1, 0, 2
    )
    head_outputs, logsum = attend(query_heads, heads_of_key, heads_of_value, allowed, factor)
    attn_own = (
        head_outputs.transpose(1, 0, 2).reshape(own_rows, QUERY_FEATURES).astype(jnp.bfloat16)
    )
    attn_cols = regroup_columns(attn_own)
    attn_proj = spread_sum(((attn_cols, out_mat),), own_rows)
    residual = inputs_f + attn_proj
    scale_two = rms_scale(residual)
    normed_two = residual * scale_two
    xn_two = (normed_two * norm2_gain).astype(jnp.bfloat16)
    xn_two_rows = gather_rows(xn_two)
    gate_pre = matmul(xn_two_rows, gate_mat)
    up_pre = matmul(xn_two_rows, up_mat)
    sigmoid_gate = jax.nn.sigmoid(gate_pre)
    hidden = (gate_pre * sigmoid_gate * up_pre).astype(jnp.bfloat16)
    mlp_proj = spread_sum(((hidden, down_mat),), own_rows)
    layer_out = (residual + mlp_proj).astype(jnp.bfloat16)
    cot_f = dealt_cot.astype(jnp.float32)
    cot_rows = gather_rows(dealt_cot)
    hidden_grad = matmul(cot_rows, down_mat)
    grad_down_part = matmul_tn(cot_rows, hidden)
    gate_grad = (
        hidden_grad * up_pre * sigmoid_gate * (1.0 + gate_pre * (1.0 - sigmoid_gate))
    ).astype(jnp.bfloat16)
    up_grad = (hidden_grad * gate_pre * sigmoid_gate).astype(jnp.bfloat16)
    xn_two_grad = spread_sum(((gate_grad, gate_mat), (up_grad, up_mat)), own_rows)
    grad_gate_part = matmul_tn(xn_two_rows, gate_grad)
    grad_up_part = matmul_tn(xn_two_rows, up_grad)
    gain_two_part = jnp.sum(xn_two_grad * normed_two, axis=0)
    normed_grad = xn_two_grad * norm2_gain
    residual_grad = cot_f + scale_two * (
        normed_grad - normed_two * jnp.mean(normed_grad * normed_two, axis=1, keepdims=True)
    )
    branch_grad = residual_grad.astype(jnp.bfloat16)
    branch_rows = gather_rows(branch_grad)
    attn_grad = regroup_tokens(matmul(branch_rows, out_mat).astype(jnp.bfloat16))
    grad_out_part = matmul_tn(branch_rows, attn_cols)
    grad_heads = attn_grad.reshape(own_rows, QUERY_HEADS, HEAD_DIMENSION).transpose(1, 0, 2)
    query_grads, key_acc, value_acc = attend_back(
        query_heads, heads_of_key, heads_of_value, grad_heads, logsum, allowed, factor
    )
    key_part = key_acc.transpose(1, 0, 2).reshape(rows_per_group, KEY_FEATURES)
    value_part = value_acc.transpose(1, 0, 2).reshape(rows_per_group, KEY_FEATURES)
    key_backward, value_back = (
        lax.psum_scatter(
            key_part.astype(jnp.bfloat16), "col", scatter_dimension=0, tiled=True
        ).astype(jnp.float32),
        lax.psum_scatter(
            value_part.astype(jnp.bfloat16), "col", scatter_dimension=0, tiled=True
        ).astype(jnp.float32),
    )
    query_back = reverse_rotation(
        query_grads.transpose(1, 0, 2).reshape(own_rows, QUERY_FEATURES),
        cosine_table,
        sine_table,
        QUERY_HEADS,
    )
    key_rotated = reverse_rotation(key_backward, cosine_table, sine_table, KEY_VALUE_HEADS)
    qkv_grad = jnp.concatenate([query_back, key_rotated, value_back], axis=1).astype(jnp.bfloat16)
    qkv_cols = regroup_columns(qkv_grad)
    xn_one_grad = spread_sum(((qkv_cols, qkv_mat),), own_rows)
    grad_qkv_part = matmul_tn(xn_one_rows, qkv_cols)
    gain_one_part = jnp.sum(xn_one_grad * normed_one, axis=0)
    normed_grad_one = xn_one_grad * norm1_gain
    input_grad = residual_grad + scale_one * (
        normed_grad_one - normed_one * jnp.mean(normed_grad_one * normed_one, axis=1, keepdims=True)
    )
    grad_qkv, grad_out, grad_gate, grad_up, grad_down = (
        lax.psum_scatter(grad_qkv_part, "row", scatter_dimension=0, tiled=True),
        lax.psum_scatter(grad_out_part, "row", scatter_dimension=0, tiled=True),
        lax.psum_scatter(grad_gate_part, "row", scatter_dimension=0, tiled=True),
        lax.psum_scatter(grad_up_part, "row", scatter_dimension=0, tiled=True),
        lax.psum_scatter(grad_down_part, "row", scatter_dimension=0, tiled=True),
    )
    grad_norm1, grad_norm2 = lax.psum((gain_one_part, gain_two_part), ("row", "col"))
    back_out, back_grad = (
        lax.all_to_all(layer_out, "row", split_axis=0, concat_axis=0, tiled=True),
        lax.all_to_all(
            input_grad.astype(jnp.bfloat16), "row", split_axis=0, concat_axis=0, tiled=True
        ),
    )
    layer_output = jnp.take(
        back_out.reshape(row_devices, block_rows, model_width), targets, axis=0
    ).reshape(own_rows, model_width)
    grad_input = jnp.take(
        back_grad.reshape(row_devices, block_rows, model_width), targets, axis=0
    ).reshape(own_rows, model_width)
    return (
        layer_output,
        grad_input,
        grad_norm1,
        grad_qkv,
        grad_out,
        grad_norm2,
        grad_gate,
        grad_up,
        grad_down,
    )


def solution(mesh):
    placed = (
        P(("row", "col"), None),
        P(),
        P("row", "col"),
        P("row", "col"),
        P(),
        P("row", "col"),
        P("row", "col"),
        P("row", "col"),
        P(("row", "col"), None),
        P("row", None),
        P(("row", "col")),
        P(("row", "col"), None),
    )
    return jax.shard_map(
        on_device,
        mesh=mesh,
        in_specs=placed,
        out_specs=(
            P(("row", "col"), None),
            P(("row", "col"), None),
            P(),
            P("row", "col"),
            P("row", "col"),
            P(),
            P("row", "col"),
            P("row", "col"),
            P("row", "col"),
        ),
        check_vma=False,
    )
```

profile of v0, /device:TPU:1, one launch (start us, length us, event | category | flops | bytes accessed | tf_op | source)
XLA Modules:
  0.0 1573.5 jit_solution(9520040302750912809)
XLA Ops:
  13.4 31.2 %all_to_all.100 = bf16[8,64,960]{2,1,0:T(8,128)(2,1)S(1)} all-to-all(bf16[8,64,960]{2,1,0:T(8,128)(2,1)S(1)} %get-tuple-element.545), channel_id=1, replica_groups=mesh['row'=8,'col'=4] {'row'}, dimensions={0} | all-to-all | bytes 1966080 | tf_op jit(solution)/shard_map/all_to_all | solution.py:197
  46.9 26.5 %all-gather = bf16[8,120,400]{1,2,0:T(8,128)(2,1)S(1)} all-gather(bf16[1,120,400]{1,2,0:T(8,128)(2,1)S(1)} %bitcast.267), channel_id=1, replica_groups=mesh['row'=8,'col'=4] {'row'}, dimensions={0}, use_global_device_ids=true | all-gather | bytes 864000 | tf_op jit(solution)/shard_map/all_gather | solution.py:201
  93.1 19.6 %all-to-all-done.1 = bf16[4,512,400]{1,2,0:T(8,128)(2,1)} async-done(((bf16[4,512,400]{1,2,0:T(8,128)(2,1)}), bf16[4,512,400]{1,2,0:T(8,128)(2,1)}, u32[]{:S(2)}, u32[]{:S(2)}) %all-to-all-start.1) | async-done | bytes 1638432 | tf_op jit(solution)/shard_map/all_to_all | solution.py:88
  121.4 11.1 all-gather.13.cloned.1.call-done
  136.3 16.6 %all-gather.15.cloned.1.call-done = bf16[2048,320]{0,1:T(8,128)(2,1)} async-done(((bf16[512,320]{0,1:T(8,128)(2,1)}), bf16[2048,320]{0,1:T(8,128)(2,1)}) %all-gather.15.cloned.1.call-update) | async-done | bytes 1310736 | tf_op jit(solution)/shard_map/all_gather | solution.py:232
  156.7 146.1 %while.34 = (s32[]{:T(128)}, bf16[15,512,64]{1,2,0:T(8,128)(2,1)}, f32[15,512]{1,0:T(8,128)}, bf16[15,512,64]{2,1,0:T(8,128)(2,1)}, s32[15]{0:T(128)S(1)}, /*ind...) while((s32[]{:T(128)}, bf16[15,512,64]{1,2,0:T(8,128)(2,1)}, ...), condition=%wide.region_8.10_spmd.clone.clone, body=%wide.region_5.9_spmd.clone.sunk.clone | while | flops 279969280 | bytes 13926677 | solution.py:122
  306.5 25.5 %all_gather.37 = bf16[960,240]{1,0:T(8,128)(2,1)S(1)} all-gather(bf16[120,240]{1,0:T(8,128)(2,1)S(1)} %copy-done.24), channel_id=1, replica_groups=mesh['row'=8,'col'=4] {'row'}, dimensions={0}, use_global_device_ids=true | all-gather | bytes 518400 | tf_op jit(solution)/shard_map/all_gather | solution.py:202
  338.5 74.6 %reduce-scatter.20.cloned.1.call-done = f32[512,960]{0,1:T(8,128)} async-done(((f32[2048,960]{0,1:T(8,128)}), f32[512,960]{0,1:T(8,128)}) %reduce-scatter.20.cloned.1.call-update) | async-done | bytes 1966096 | tf_op jit(solution)/shard_map/reduce_scatter | solution.py:99
  419.1 30.1 %all_to_all.101 = bf16[8,64,960]{2,1,0:T(8,128)(2,1)} all-to-all(bf16[8,64,960]{2,1,0:T(8,128)(2,1)S(1)} %copy-done.8), channel_id=1, replica_groups=mesh['row'=8,'col'=4] {'row'}, dimensions={0} | all-to-all | bytes 1966080 | tf_op jit(solution)/shard_map/all_to_all | solution.py:198
  451.0 8.3 fusion.50
  459.4 33.9 %all-gather.19.cloned.1.call-done = bf16[960,640]{1,0:T(8,128)(2,1)} async-done(((bf16[120,640]{1,0:T(8,128)(2,1)}), bf16[960,640]{1,0:T(8,128)(2,1)}) %all-gather.19.cloned.1.call-update) | async-done | bytes 1228816 | tf_op jit(solution)/shard_map/all_gather | solution.py:203
  493.3 8.3 fusion.49
  501.6 34.6 %all-gather.23.cloned.1.call-done = bf16[960,640]{1,0:T(8,128)(2,1)} async-done(((bf16[120,640]{1,0:T(8,128)(2,1)}), bf16[960,640]{1,0:T(8,128)(2,1)}) %all-gather.23.cloned.1.call-update) | async-done | bytes 1228816 | tf_op jit(solution)/shard_map/all_gather | solution.py:205
  536.2 36.5 %all-gather.25.cloned.1.call-done = bf16[2048,960]{1,0:T(8,128)(2,1)} async-done(((bf16[512,960]{1,0:T(8,128)(2,1)}), bf16[2048,960]{1,0:T(8,128)(2,1)}) %all-gather.25.cloned.1.call-update) | async-done | bytes 3932176 | tf_op jit(solution)/shard_map/all_gather | solution.py:84
  572.7 10.5 multiply_convert_fusion.1
  594.3 66.0 %reduce-scatter.24.cloned.1.call-done = f32[512,960]{0,1:T(8,128)} async-done(((f32[2048,960]{0,1:T(8,128)}), f32[512,960]{0,1:T(8,128)}) %reduce-scatter.24.cloned.1.call-update) | async-done | bytes 1966096 | tf_op jit(solution)/shard_map/reduce_scatter | solution.py:99
  664.1 33.7 %all-gather.27.cloned.1.call-done = bf16[2048,960]{0,1:T(8,128)(2,1)} async-done(((bf16[512,960]{0,1:T(8,128)(2,1)}), bf16[2048,960]{0,1:T(8,128)(2,1)}) %all-gather.27.cloned.1.call-update) | async-done | bytes 3932176 | tf_op jit(solution)/shard_map/all_gather | solution.py:84
  705.9 12.9 all-to-all-done.5
  721.8 236.4 %while.35 = (s32[]{:T(128)}, f32[5,2048,64]{1,2,0:T(8,128)}, f32[5,2048,64]{1,2,0:T(8,128)S(1)}, f32[15,512,64]{1,2,0:T(8,128)}, s32[15]{0:T(128)S(1)}, /*index=...) while((s32[]{:T(128)}, f32[5,2048,64]{1,2,0:T(8,128)}, ...), condition=%wide.region_16.18_spmd.clone.clone, body=%wide.region_14.17_spmd.clone.sunk.clone | while | flops 684097024 | bytes 37771592 | solution.py:162
  964.6 23.5 %reduce-scatter.26.cloned.1.call-done = bf16[512,320]{0,1:T(8,128)(2,1)} async-done(((bf16[2048,320]{0,1:T(8,128)(2,1)}), bf16[512,320]{0,1:T(8,128)(2,1)}) %reduce-scatter.26.cloned.1.call-update) | async-done | bytes 327696 | tf_op jit(solution)/shard_map/reduce_scatter | solution.py:292
  989.3 28.1 %reduce-scatter.28.cloned.1.call-done = bf16[512,320]{0,1:T(8,128)(2,1)} async-done(((bf16[2048,320]{0,1:T(8,128)(2,1)}), bf16[512,320]{0,1:T(8,128)(2,1)}) %reduce-scatter.28.cloned.1.call-update) | async-done | bytes 327696 | tf_op jit(solution)/shard_map/reduce_scatter | solution.py:295
  1018.5 23.3 %all_to_all.102 = bf16[512,4,400]{0,2,1:T(8,128)(2,1)S(1)} all-to-all(bf16[512,4,400]{0,2,1:T(8,128)(2,1)S(1)} %bitcast.241), channel_id=1, replica_groups=mesh['row'=8,'col'=4] {'col'}, dimensions={1} | all-to-all | bytes 3276800 | tf_op jit(solution)/shard_map/all_to_all | solution.py:92
  1071.5 8.1 fusion.56
  1086.6 29.7 %reduce-scatter.30.cloned.1.call-done = f32[512,960]{0,1:T(8,128)} async-done(((f32[2048,960]{0,1:T(8,128)}), f32[512,960]{0,1:T(8,128)}) %reduce-scatter.30.cloned.1.call-update) | async-done | bytes 1966096 | tf_op jit(solution)/shard_map/reduce_scatter | solution.py:99
  1118.5 69.3 %reduce-scatter.22.cloned.1.call-done = f32[512,960]{0,1:T(8,128)} async-done(((f32[2048,960]{0,1:T(8,128)}), f32[512,960]{0,1:T(8,128)}) %reduce-scatter.22.cloned.1.call-update) | async-done | bytes 1966096 | tf_op jit(solution)/shard_map/reduce_scatter | solution.py:99
  1201.6 37.8 %all-to-all-done.7 = bf16[8,64,960]{2,1,0:T(8,128)(2,1)S(1)} async-done(((bf16[8,64,960]{2,1,0:T(8,128)(2,1)}), bf16[8,64,960]{2,1,0:T(8,128)(2,1)S(1)}, u32[]{:S(2)}, u32[]{:S(2)}) %all-to-all-start.7) | async-done | bytes 983072 | tf_op jit(solution)/shard_map/all_to_all | solution.py:325
  1247.6 30.1 %reduce-scatter.34.cloned.1.call-done = f32[120,400]{1,0:T(8,128)} async-done(((f32[960,400]{1,0:T(8,128)}), f32[120,400]{1,0:T(8,128)}) %reduce-scatter.34.cloned.1.call-update) | async-done | bytes 192016
  1279.5 41.3 %all-reduce.3 = (f32[960]{0:T(1024)}, f32[960]{0:T(1024)}) all-reduce(f32[960]{0:T(1024)S(1)} %get-tuple-element.467, f32[960]{0:T(1024)S(1)} %get-tuple-element.465), channel_id=1, replica_groups=mesh['row'=8,'col'=4] {'row','col'}, use_global_device_ids=true, to_apply=%region_22.24 | all-reduce | flops 1920 | bytes 15360 | tf_op jit(solution)/shard_map/psum | solution.py:322
  1326.8 25.5 %reduce-scatter.40.cloned.1.call-done = f32[120,640]{1,0:T(8,128)} async-done(((f32[960,640]{1,0:T(8,128)}), f32[120,640]{1,0:T(8,128)}) %reduce-scatter.40.cloned.1.call-update) | async-done | bytes 307216
  1352.3 73.8 %reduce-scatter.36.cloned.1.call-done = f32[120,640]{1,0:T(8,128)} async-done(((f32[960,640]{1,0:T(8,128)}), f32[120,640]{1,0:T(8,128)}) %reduce-scatter.36.cloned.1.call-update) | async-done | bytes 307216
  1426.1 73.1 %reduce-scatter.38.cloned.1.call-done = f32[120,640]{1,0:T(8,128)} async-done(((f32[960,640]{1,0:T(8,128)}), f32[120,640]{1,0:T(8,128)}) %reduce-scatter.38.cloned.1.call-update) | async-done | bytes 307216
  1499.3 66.2 %reduce-scatter.32.cloned.1.call-done = f32[120,240]{1,0:T(8,128)} async-done(((f32[960,240]{1,0:T(8,128)}), f32[120,240]{1,0:T(8,128)}) %reduce-scatter.32.cloned.1.call-update) | async-done | bytes 115216 | tf_op jit(solution)/shard_map/reduce_scatter | solution.py:317
  (430 shorter events, 487.2 us)
Async XLA Ops:
  8.0 72.6 %all-gather.11.cloned.1.call-start = ((), (), s32[]{:S(2)}) async-start(), calls=%async_computation.19 | async-start | bytes 4915200 | tf_op jit(solution)/shard_map/all_gather | solution.py:84
  45.5 367.6 %copy-start = (f32[512,960]{0,1:T(8,128)}, f32[512,960]{0,1:T(8,128)S(1)}, u32[]{:S(2)}) copy-start(f32[512,960]{0,1:T(8,128)S(1)} %copy.93) | copy-start | bytes 5898244
  86.2 26.5 %all-to-all-start.1 = ((bf16[4,512,400]{1,2,0:T(8,128)(2,1)}), bf16[4,512,400]{1,2,0:T(8,128)(2,1)}, u32[]{:S(2)}, u32[]{:S(2)}) async-start(bf16[4,512,400]{1,2,0:T(8,128)(2,1)} %bitcast.240), calls=%async_computation.1 | async-start | bytes 3276800 | tf_op jit(solution)/shard_map/all_to_all | solution.py:88
  92.7 39.8 %all-gather.13.cloned.1.call-start = ((), (), s32[]{:S(2)}) async-start(), calls=%async_computation.20 | async-start | bytes 1638400 | tf_op jit(solution)/shard_map/all_gather | solution.py:231
  115.5 37.4 %all-gather.15.cloned.1.call-start = ((), (), s32[]{:S(2)}) async-start(), calls=%async_computation.21 | async-start | bytes 1638400 | tf_op jit(solution)/shard_map/all_gather | solution.py:232
  156.7 149.8 %copy-start.24 = (bf16[120,240]{1,0:T(8,128)(2,1)S(1)}, bf16[120,240]{1,0:T(8,128)(2,1)}, u32[]{:S(2)}) copy-start(bf16[120,240]{1,0:T(8,128)(2,1)} %param.21) | copy-start | bytes 172804
  302.8 29.2 %all-to-all-start.2 = ((bf16[512,4,240]{0,2,1:T(8,128)(2,1)}), bf16[512,4,240]{0,2,1:T(8,128)(2,1)S(1)}, u32[]{:S(2)}, u32[]{:S(2)}) async-start(bf16[512,4,240]{0,2,1:T(8,128)(2,1)} %bitcast.20), calls=%async_computation.2 | async-start | bytes 1966080 | tf_op jit(solution)/shard_map/all_to_all | solution.py:92
  306.5 106.6 %reduce-scatter.20.cloned.1.call-start = ((), (), s32[]{:S(2)}) async-start(), calls=%async_computation.22 | async-start | bytes 9830400 | tf_op jit(solution)/shard_map/reduce_scatter | solution.py:99
  337.4 111.8 %all-gather.21.cloned.1.call-start = ((), (), s32[]{:S(2)}) async-start(), calls=%async_computation.25 | async-start | bytes 1382400 | tf_op jit(solution)/shard_map/all_gather | solution.py:204
  338.0 78.5 %copy-start.23 = (f32[960]{0:T(1024)S(1)}, f32[960]{0:T(1024)}, u32[]{:S(2)}) copy-start(f32[960]{0:T(1024)} %param.22) | copy-start | bytes 11524
  338.0 113.1 %all-gather.17.cloned.1.call-start = ((), (), s32[]{:S(2)}) async-start(), calls=%async_computation.23 | async-start | bytes 4915200 | tf_op jit(solution)/shard_map/all_gather | solution.py:84
  417.7 75.6 %all-gather.19.cloned.1.call-start = ((), (), s32[]{:S(2)}) async-start(), calls=%async_computation.24 | async-start | bytes 1382400 | tf_op jit(solution)/shard_map/all_gather | solution.py:203
  418.3 117.9 %all-gather.23.cloned.1.call-start = ((), (), s32[]{:S(2)}) async-start(), calls=%async_computation.26 | async-start | bytes 1382400 | tf_op jit(solution)/shard_map/all_gather | solution.py:205
  419.0 153.7 %all-gather.25.cloned.1.call-start = ((), (), s32[]{:S(2)}) async-start(), calls=%async_computation.28 | async-start | bytes 5242880 | tf_op jit(solution)/shard_map/all_gather | solution.py:84
  449.1 211.2 %reduce-scatter.24.cloned.1.call-start = ((), (), s32[]{:S(2)}) async-start(), calls=%async_computation.29 | async-start | bytes 9830400 | tf_op jit(solution)/shard_map/reduce_scatter | solution.py:99
  501.6 81.5 %copy-start.31 = (bf16[960,640]{1,0:T(8,128)(2,1)S(1)}, bf16[960,640]{1,0:T(8,128)(2,1)}, u32[]{:S(2)}) copy-start(bf16[960,640]{1,0:T(8,128)(2,1)} %all-gather.19.cloned.1.call-done) | copy-start | bytes 3686404
  591.8 68.5 %copy-start.3 = (f32[512,960]{0,1:T(8,128)S(1)}, f32[512,960]{0,1:T(8,128)}, u32[]{:S(2)}) copy-start(f32[512,960]{0,1:T(8,128)} %copy-done.2) | copy-start | bytes 5898244
  591.9 105.9 %all-gather.27.cloned.1.call-start = ((), (), s32[]{:S(2)}) async-start(), calls=%async_computation.30 | async-start | bytes 4915200 | tf_op jit(solution)/shard_map/all_gather | solution.py:84
  594.3 68.3 %copy-start.6 = (bf16[512,960]{0,1:T(8,128)(2,1)S(1)}, bf16[512,960]{0,1:T(8,128)(2,1)}, u32[]{:S(2)}) copy-start(bf16[512,960]{0,1:T(8,128)(2,1)} %copy.96) | copy-start | bytes 2949124
  702.1 16.6 %all-to-all-start.5 = ((bf16[4,512,240]{1,2,0:T(8,128)(2,1)}), bf16[4,512,240]{1,2,0:T(8,128)(2,1)S(1)}, u32[]{:S(2)}, u32[]{:S(2)}) async-start(bf16[4,512,240]{1,2,0:T(8,128)(2,1)} %bitcast.164), calls=%async_computation.8 | async-start | bytes 1966080 | tf_op jit(solution)/shard_map/all_to_all | solution.py:88
  705.9 282.3 %reduce-scatter.26.cloned.1.call-start = ((), (), s32[]{:S(2)}) async-start(), calls=%async_computation.31 | async-start | bytes 1638400 | tf_op jit(solution)/shard_map/reduce_scatter | solution.py:292
  961.3 56.1 %reduce-scatter.28.cloned.1.call-start = ((), (), s32[]{:S(2)}) async-start(), calls=%async_computation.32 | async-start | bytes 1638400 | tf_op jit(solution)/shard_map/reduce_scatter | solution.py:295
  962.7 153.7 %reduce-scatter.30.cloned.1.call-start = ((), (), s32[]{:S(2)}) async-start(), calls=%async_computation.33 | async-start | bytes 9830400 | tf_op jit(solution)/shard_map/reduce_scatter | solution.py:99
  1047.3 140.4 %reduce-scatter.22.cloned.1.call-start = ((), (), s32[]{:S(2)}) async-start(), calls=%async_computation.27 | async-start | bytes 9830400 | tf_op jit(solution)/shard_map/reduce_scatter | solution.py:99
  1056.6 221.2 %reduce-scatter.34.cloned.1.call-start = ((), (), s32[]{:S(2)}) async-start(), calls=%async_computation.35 | async-start | bytes 2211840
  1063.2 289.1 %reduce-scatter.40.cloned.1.call-start = ((), (), s32[]{:S(2)}) async-start(), calls=%async_computation.38 | async-start | bytes 2764800
  1071.5 354.7 %reduce-scatter.36.cloned.1.call-start = ((), (), s32[]{:S(2)}) async-start(), calls=%async_computation.36 | async-start | bytes 2764800
  1079.7 419.6 %reduce-scatter.38.cloned.1.call-start = ((), (), s32[]{:S(2)}) async-start(), calls=%async_computation.37 | async-start | bytes 2764800
  1086.5 101.2 %copy-start.7 = (bf16[512,960]{0,1:T(8,128)(2,1)S(1)}, bf16[512,960]{0,1:T(8,128)(2,1)}, u32[]{:S(2)}) copy-start(bf16[512,960]{0,1:T(8,128)(2,1)} %copy.96) | copy-start | bytes 2949124
  1194.9 44.5 %all-to-all-start.7 = ((bf16[8,64,960]{2,1,0:T(8,128)(2,1)}), bf16[8,64,960]{2,1,0:T(8,128)(2,1)S(1)}, u32[]{:S(2)}, u32[]{:S(2)}) async-start(bf16[8,64,960]{2,1,0:T(8,128)(2,1)} %bitcast.42), calls=%async_computation.13 | async-start | bytes 2097152 | tf_op jit(solution)/shard_map/all_to_all | solution.py:325
  1239.4 82.0 %all-to-all-start.3 = ((bf16[8,64,960]{2,1,0:T(8,128)(2,1)}), bf16[8,64,960]{2,1,0:T(8,128)(2,1)S(1)}, u32[]{:S(2)}, u32[]{:S(2)}) async-start(bf16[8,64,960]{2,1,0:T(8,128)(2,1)} %bitcast.22), calls=%async_computation.5 | async-start | bytes 2097152 | tf_op jit(solution)/shard_map/all_to_all | solution.py:324
  1243.1 322.4 %reduce-scatter.32.cloned.1.call-start = ((), (), s32[]{:S(2)}) async-start(), calls=%async_computation.34 | async-start | bytes 1105920 | tf_op jit(solution)/shard_map/reduce_scatter | solution.py:317
  (28 other events, 341.6 us)
Sparse Core Ops, SparseCore 0:
  47.0 33.5 all-gather.10
  115.7 16.8 all-gather.12
  134.7 18.1 all-gather.14
  337.5 75.5 reduce-scatter.19
  664.2 33.4 all-gather.26
  961.4 26.7 reduce-scatter.25
  990.8 26.5 reduce-scatter.27
Sparse Core Ops, SparseCore 1:
  340.1 46.9 all-gather.20
  417.8 33.2 all-gather.16
  453.3 39.9 all-gather.18
  495.8 40.4 all-gather.22
  537.8 34.8 all-gather.24
  591.9 68.3 reduce-scatter.23
  1047.4 68.8 reduce-scatter.29
  1118.9 68.8 reduce-scatter.21
  1191.1 86.5 reduce-scatter.33
  1282.4 69.9 reduce-scatter.39
  1356.8 69.2 reduce-scatter.35
  1430.8 68.4 reduce-scatter.37
  1503.4 62.0 reduce-scatter.31
where the time goes:
time: 1590 us; the launch traced here: 1570 us
  waiting for transfers between devices  807 us (51%)
  matrix products  335 us (21%)
  blocking collectives  178 us (11%)
  local copies, waits for them, and re-layouts  105 us (7%)
  loops' own time  59.7 us (4%)
  other arithmetic  47.7 us (3%)
  starting transfers between devices  24.6 us (2%)
  between operations  17 us (1%)
    reduce_scatter x4, waiting for transfers between devices, spread_sum(): return lax.psum_scatter(result, 'col', scatter_dimension=0, tiled=True)  240 us
    unnamed x24, waiting for transfers between devices  205 us
    dot_general x50, matrix products, matmul_nt(): lax.dot_general(left_mat, right_mat, (((1,), (1,)), ((), ())), preferred_...  134 us
    dot_general x35, matrix products, matmul(): return jnp.dot(left_mat, right_mat, preferred_element_type=jnp.float32)  113 us
    dot_general x34, matrix products, matmul_tn(): lax.dot_general(left_mat, right_mat, (((0,), (0,)), ((), ())), preferred_...  81 us
    all_gather x4, waiting for transfers between devices, gather_rows(): return lax.all_gather(values, 'col', axis=0, tiled=True)  77.5 us
    reduce_scatter x1, waiting for transfers between devices, on_device(): lax.psum_scatter(grad_out_part, 'row', scatter_dimension=0, tiled=True)  66.2 us
    psum x1, blocking collectives, on_device(): lax.psum((gain_one_part, gain_two_part), ('row', 'col'))  41.3 us
  transfers between devices with their start and end apart: 25, of which 22 were waited for; matrix products, arithmetic and copies ran while one was open for 6% of the time, Pallas kernels for 0%

commit v1 on v0

v1 whole, which is shorter than its diff:
```python
import math
import functools

import jax
import jax.numpy as jnp
from jax import lax
from jax.experimental import pallas as pl
from jax.experimental.pallas import tpu as pltpu
from jax.sharding import PartitionSpec as P

QUERY_HEADS = 15
KEY_VALUE_HEADS = 5
HEADS_PER_GROUP = 3
HEAD_DIMENSION = 64
QUERY_FEATURES = 960
KEY_FEATURES = 320
LONGEST = 1024

EPS = 1e-05
NEG_FILL = -1e30
THETA = 10000.0
LANES = 128
TILE = 256
VMEM_BYTES = 60 << 20

F32 = jnp.float32
BF16 = jnp.bfloat16


def nn(left_mat, right_mat):
    return jnp.dot(left_mat, right_mat, preferred_element_type=F32)


def nt(left_mat, right_mat):
    return lax.dot_general(
        left_mat, right_mat, (((1,), (1,)), ((), ())), preferred_element_type=F32
    )


def lane_ids(rows):
    return lax.broadcasted_iota(jnp.int32, (rows, LANES), 1)


def keep_low(values):
    return jnp.where(lane_ids(values.shape[0]) < HEAD_DIMENSION, values, 0.0)


def keep_high(values):
    return jnp.where(lane_ids(values.shape[0]) >= HEAD_DIMENSION, values, 0.0)


def swap_halves(values):
    return pltpu.roll(values, HEAD_DIMENSION, 1)


def turn(values, cosine, sine):
    ids = lane_ids(values.shape[0])
    first = lax.rem(ids, HEAD_DIMENSION) < HEAD_DIMENSION // 2
    ahead = pltpu.roll(values, LANES - HEAD_DIMENSION // 2, 1)
    behind = pltpu.roll(values, HEAD_DIMENSION // 2, 1)
    return values * cosine + jnp.where(first, ahead, behind) * sine


def rms_scale(values):
    return lax.rsqrt(jnp.mean(values * values, axis=1, keepdims=True) + EPS)


def full_spec(shape):
    return pl.BlockSpec(shape, lambda *_: (0,) * len(shape))


def project_kernel(x_ref, gain_ref, w_ref, cos_ref, sin_ref, q_ref, kv_ref, rows_scr):
    own_rows = x_ref.shape[0]
    width = w_ref.shape[0]
    block = QUERY_FEATURES + 2 * KEY_FEATURES
    block = block // width
    inputs_f = x_ref[...].astype(F32)
    xn = (inputs_f * rms_scale(inputs_f) * gain_ref[...]).astype(BF16)
    for c in range(width):
        part = nn(xn, w_ref[c, :, :block])
        rows_scr[:, c * block : (c + 1) * block] = part.astype(BF16).astype(F32)
    half_rows = own_rows // 2
    turned = []
    for p in range(13):
        chunk = rows_scr[:, p * LANES : (p + 1) * LANES]
        if p < 10:
            chunk = turn(chunk, cos_ref[...], sin_ref[...])
        turned.append(chunk)
        for half in range(2):
            h = 2 * p + half
            if h < QUERY_HEADS:
                piece = chunk if half == 0 else swap_halves(chunk)
                piece = keep_low(piece.astype(BF16).astype(F32) * 0.125).astype(BF16)
                g, j = divmod(h, HEADS_PER_GROUP)
                for b in range(2):
                    q_ref[g, b, j * half_rows : (j + 1) * half_rows, :] = piece[
                        b * half_rows : (b + 1) * half_rows
                    ]
    for g in range(KEY_VALUE_HEADS):
        k_piece = QUERY_HEADS + g
        v_piece = QUERY_HEADS + KEY_VALUE_HEADS + g
        key = turned[k_piece // 2]
        key = key if k_piece % 2 == 0 else swap_halves(key)
        value = turned[v_piece // 2]
        value = value if v_piece % 2 == 1 else swap_halves(value)
        ids = lane_ids(own_rows)
        kv_ref[g] = jnp.where(ids < HEAD_DIMENSION, key, value).astype(BF16)


def project(x, gain, w_a, cosine, sine):
    own_rows, model_width = x.shape
    width = w_a.shape[0]
    q_shape = (KEY_VALUE_HEADS, 2, HEADS_PER_GROUP * own_rows // 2, LANES)
    kv_shape = (KEY_VALUE_HEADS, own_rows, LANES)
    return pl.pallas_call(
        project_kernel,
        grid=(1,),
        out_shape=(
            jax.ShapeDtypeStruct(q_shape, BF16),
            jax.ShapeDtypeStruct(kv_shape, BF16),
        ),
        in_specs=[
            full_spec(x.shape),
            full_spec(gain.shape),
            pl.BlockSpec((width, model_width, 512), lambda i: (0, 0, 0)),
            full_spec(cosine.shape),
            full_spec(sine.shape),
        ],
        out_specs=(full_spec(q_shape), full_spec(kv_shape)),
        scratch_shapes=[pltpu.VMEM((own_rows, 13 * LANES), F32)],
        compiler_params=pltpu.CompilerParams(vmem_limit_bytes=VMEM_BYTES),
        name="project",
    )(x, gain, w_a, cosine, sine)


def fill_bias(low_ref, start_ref, bias_scr):
    half_rows = bias_scr.shape[2]
    for b in range(2):
        starts = start_ref[b * half_rows : (b + 1) * half_rows, :]
        ids = lax.broadcasted_iota(jnp.int32, (half_rows, LANES), 1)
        own = lax.broadcasted_iota(jnp.int32, (half_rows, LANES), 0) + (
            LONGEST + b * half_rows
        )

        def one_tile(t, carry, b=b, starts=starts, ids=ids, own=own):
            for part in range(TILE // LANES):
                keys = ids + (t * TILE + part * LANES)
                allowed = (keys >= starts) & (keys <= own)
                bias_scr[b, t, :, part * LANES : (part + 1) * LANES] = jnp.where(
                    allowed, 0.0, NEG_FILL
                )
            return carry

        lax.fori_loop(low_ref[b], 5 + b, one_tile, 0)


def attend_kernel(low_ref, start_ref, q_ref, kv_ref, o_ref, logsum_ref, bias_scr, s_scr, m_scr, acc_scr):
    half_rows = bias_scr.shape[2]

    @pl.when(pl.program_id(0) == 0)
    def _():
        fill_bias(low_ref, start_ref, bias_scr)

    ones = jnp.ones((TILE, LANES), BF16)
    for b in range(2):
        low, high = low_ref[b], 5 + b
        m_scr[...] = jnp.full(m_scr.shape, -3e38, F32)

        def scores_of(t, carry, b=b):
            keys = kv_ref[0, pl.ds(pl.multiple_of(t * TILE, TILE), TILE), :]
            s = nt(q_ref[0, b], keys)
            bias = bias_scr[b, t]
            for j in range(HEADS_PER_GROUP):
                rows = slice(j * half_rows, (j + 1) * half_rows)
                part = s[rows] + bias
                s_scr[t, rows, :] = part
                m_scr[rows, :] = jnp.maximum(
                    m_scr[rows, :], jnp.maximum(part[:, :LANES], part[:, LANES:])
                )
            return carry

        lax.fori_loop(low, high, scores_of, 0)
        row_max = jnp.max(m_scr[...], axis=1, keepdims=True)
        acc_scr[...] = jnp.zeros_like(acc_scr)

        def weigh(t, carry, row_max=row_max):
            keys = kv_ref[0, pl.ds(pl.multiple_of(t * TILE, TILE), TILE), :]
            p = jnp.exp(s_scr[t] - row_max).astype(BF16)
            acc_scr[...] += nn(p, jnp.concatenate([keys, ones], axis=1))
            return carry

        lax.fori_loop(low, high, weigh, 0)
        total = acc_scr[:, LANES:]
        o_ref[0, b] = keep_high(acc_scr[:, :LANES] / total).astype(BF16)
        logsum_ref[0, b] = row_max + jnp.log(total)


def attend(low, start, q, kv):
    groups, blocks, rows, lanes = q.shape
    half_rows = rows // HEADS_PER_GROUP
    window = kv.shape[1]
    q_spec = pl.BlockSpec((1, blocks, rows, lanes), lambda g: (g, 0, 0, 0))
    return pl.pallas_call(
        attend_kernel,
        grid=(groups,),
        out_shape=(
            jax.ShapeDtypeStruct(q.shape, BF16),
            jax.ShapeDtypeStruct(q.shape, F32),
        ),
        in_specs=[
            pl.BlockSpec(memory_space=pltpu.SMEM),
            full_spec(start.shape),
            q_spec,
            pl.BlockSpec((1, window, lanes), lambda g: (g, 0, 0)),
        ],
        out_specs=(q_spec, q_spec),
        scratch_shapes=[
            pltpu.VMEM((2, window // TILE, half_rows, TILE), F32),
            pltpu.VMEM((window // TILE, rows, TILE), F32),
            pltpu.VMEM((rows, lanes), F32),
            pltpu.VMEM((rows, TILE), F32),
        ],
        compiler_params=pltpu.CompilerParams(vmem_limit_bytes=VMEM_BYTES),
        name="attend",
    )(low, start, q, kv)


def attend_back_kernel(
    low_ref, start_ref, q_ref, kv_ref, o_ref, do_ref, logsum_ref, dq_ref, dkv_ref, bias_scr, acc_scr, dq_scr
):
    half_rows = bias_scr.shape[2]

    @pl.when(pl.program_id(0) == 0)
    def _():
        fill_bias(low_ref, start_ref, bias_scr)

    acc_scr[...] = jnp.zeros_like(acc_scr)
    for b in range(2):
        low, high = low_ref[b], 5 + b
        delta = jnp.sum(
            o_ref[0, b].astype(F32) * do_ref[0, b].astype(F32), axis=1, keepdims=True
        )
        q_t = q_ref[0, b].T
        do_t = do_ref[0, b].T
        dq_scr[...] = jnp.zeros_like(dq_scr)

        def one_tile(t, carry, b=b, delta=delta, q_t=q_t, do_t=do_t):
            keys = kv_ref[0, pl.ds(pl.multiple_of(t * TILE, TILE), TILE), :]
            bias = bias_scr[b, t]
            s = nt(q_ref[0, b], keys)
            dp = nt(do_ref[0, b], keys)
            ds_parts, p_parts = [], []
            for j in range(HEADS_PER_GROUP):
                rows = slice(j * half_rows, (j + 1) * half_rows)
                sub = logsum_ref[0, b, rows, :]
                p = jnp.exp(s[rows] + bias - jnp.concatenate([sub, sub], axis=1))
                ds_parts.append((p * (dp[rows] - delta[rows])).astype(BF16))
                p_parts.append(p.astype(BF16))
            ds = jnp.concatenate(ds_parts, axis=0)
            p_low = jnp.concatenate(p_parts, axis=0)
            dq_scr[...] += nn(ds, keys)
            acc_scr[t] += nn(q_t, ds) + nn(do_t, p_low)
            return carry

        lax.fori_loop(low, high, one_tile, 0)
        dq_ref[0, b] = dq_scr[...]
    for t in range(acc_scr.shape[0]):
        dkv_ref[0, t * TILE : (t + 1) * TILE, :] = acc_scr[t].T.astype(BF16)


def attend_back(low, start, q, kv, o, do, logsum):
    groups, blocks, rows, lanes = q.shape
    half_rows = rows // HEADS_PER_GROUP
    window = kv.shape[1]
    q_spec = pl.BlockSpec((1, blocks, rows, lanes), lambda g: (g, 0, 0, 0))
    kv_spec = pl.BlockSpec((1, window, lanes), lambda g: (g, 0, 0))
    return pl.pallas_call(
        attend_back_kernel,
        grid=(groups,),
        out_shape=(
            jax.ShapeDtypeStruct(q.shape, F32),
            jax.ShapeDtypeStruct(kv.shape, BF16),
        ),
        in_specs=[
            pl.BlockSpec(memory_space=pltpu.SMEM),
            full_spec(start.shape),
            q_spec,
            kv_spec,
            q_spec,
            q_spec,
            q_spec,
        ],
        out_specs=(q_spec, kv_spec),
        scratch_shapes=[
            pltpu.VMEM((2, window // TILE, half_rows, TILE), F32),
            pltpu.VMEM((window // TILE, lanes, TILE), F32),
            pltpu.VMEM((rows, lanes), F32),
        ],
        compiler_params=pltpu.CompilerParams(vmem_limit_bytes=VMEM_BYTES),
        name="attend_back",
    )(low, start, q, kv, o, do, logsum)


def middle_kernel(
    x_ref,
    o_ref,
    cot_ref,
    gain_ref,
    wo_ref,
    w_ref,
    g_ref,
    out_ref,
    rg_ref,
    do_ref,
    go_ref,
    gain_grad_ref,
    attn_scr,
    wide_scr,
    xn_scr,
    xn_t_scr,
    cot_t_scr,
    res_scr,
    scale_scr,
    mlp_scr,
    xg_scr,
    hid_scr,
    gg_scr,
    ug_scr,
):
    step = pl.program_id(0)
    width = wo_ref.shape[0]
    own_rows = x_ref.shape[0]
    half_rows = own_rows // 2
    block = QUERY_FEATURES // width
    model_width = x_ref.shape[1]

    @pl.when(step == 0)
    def _():
        for p in range(8):
            for b in range(2):
                rows = slice(b * half_rows, (b + 1) * half_rows)
                g, j = divmod(2 * p, HEADS_PER_GROUP)
                pair = swap_halves(
                    o_ref[g, b, j * half_rows : (j + 1) * half_rows, :].astype(F32)
                )
                if 2 * p + 1 < QUERY_HEADS:
                    g, j = divmod(2 * p + 1, HEADS_PER_GROUP)
                    pair = pair + o_ref[
                        g, b, j * half_rows : (j + 1) * half_rows, :
                    ].astype(F32)
                attn_scr[rows, p * LANES : (p + 1) * LANES] = pair.astype(BF16)
        residual = x_ref[...].astype(F32)
        for c in range(width):
            residual = residual + nt(
                attn_scr[:, c * block : (c + 1) * block], wo_ref[c, :, :block]
            )
        scale = rms_scale(residual)
        scale_scr[...] = scale
        res_scr[...] = residual
        xn = (residual * scale * gain_ref[...]).astype(BF16)
        xn_scr[...] = xn
        xn_t_scr[...] = xn.T
        cot_t_scr[...] = cot_ref[...].T
        mlp_scr[...] = jnp.zeros_like(mlp_scr)
        xg_scr[...] = jnp.zeros_like(xg_scr)

    def one_part(i, carry):
        rows = pl.ds(pl.multiple_of(i * half_rows, half_rows), half_rows)
        xn = xn_scr[rows, :]
        gate = nn(xn, w_ref[0, 0])
        up = nn(xn, w_ref[0, 1])
        hid_grad = nn(cot_ref[rows, :], w_ref[0, 2])
        sig = 1.0 / (1.0 + jnp.exp(-gate))
        act = gate * sig
        hid = (act * up).astype(BF16)
        gg = (hid_grad * up * sig * (1.0 + gate * (1.0 - sig))).astype(BF16)
        ug = (hid_grad * act).astype(BF16)
        hid_scr[rows, :] = hid
        gg_scr[rows, :] = gg
        ug_scr[rows, :] = ug
        mlp_scr[rows, :] += nt(hid, w_ref[0, 2])
        xg_scr[rows, :] += nt(gg, w_ref[0, 0]) + nt(ug, w_ref[0, 1])
        return carry

    lax.fori_loop(0, 2, one_part, 0)

    part_rows = model_width // 4

    def one_grad(i, carry):
        rows = pl.ds(pl.multiple_of(i * part_rows, 16), part_rows)
        xn_t = xn_t_scr[rows, :]
        g_ref[0, 0, rows, :] = nn(xn_t, gg_scr[...]).astype(BF16)
        g_ref[0, 1, rows, :] = nn(xn_t, ug_scr[...]).astype(BF16)
        g_ref[0, 2, rows, :] = nn(cot_t_scr[rows, :], hid_scr[...]).astype(BF16)
        return carry

    lax.fori_loop(0, 4, one_grad, 0)

    @pl.when(step == pl.num_programs(0) - 1)
    def _():
        residual = res_scr[...]
        scale = scale_scr[...]
        out_ref[...] = (residual + mlp_scr[...]).astype(BF16)
        normed = residual * scale
        xg = xg_scr[...]
        gain_grad_ref[...] = jnp.sum(xg * normed, axis=0, keepdims=True)
        e = xg * gain_ref[...]
        rg = cot_ref[...].astype(F32) + scale * (
            e - normed * jnp.mean(e * normed, axis=1, keepdims=True)
        )
        rg_ref[...] = rg
        branch = rg.astype(BF16)
        branch_t = branch.T
        for c in range(width):
            wide_scr[:, c * block : (c + 1) * block] = (
                nn(branch, wo_ref[c, :, :block]).astype(BF16).astype(F32)
            )
            go_ref[c, :, :block] = nn(
                branch_t, attn_scr[:, c * block : (c + 1) * block]
            ).astype(BF16)
            go_ref[c, :, block:] = jnp.zeros((model_width, go_ref.shape[2] - block), BF16)
        for h in range(QUERY_HEADS):
            g, j = divmod(h, HEADS_PER_GROUP)
            p, half = divmod(h, 2)
            piece = wide_scr[:, p * LANES : (p + 1) * LANES]
            piece = keep_high(piece if half == 1 else swap_halves(piece)).astype(BF16)
            for b in range(2):
                do_ref[g, b, j * half_rows : (j + 1) * half_rows, :] = piece[
                    b * half_rows : (b + 1) * half_rows
                ]


def middle(x, o, cot, gain, w_a, w_b):
    own_rows, model_width = x.shape
    width, kinds, _, block = w_b.shape
    row_spec = full_spec(x.shape)
    rows_f32 = pltpu.VMEM((own_rows, model_width), F32)
    w_spec = pl.BlockSpec((1, kinds, model_width, block), lambda c: (c, 0, 0, 0))
    return pl.pallas_call(
        middle_kernel,
        grid=(width,),
        out_shape=(
            jax.ShapeDtypeStruct(w_b.shape, BF16),
            jax.ShapeDtypeStruct(x.shape, BF16),
            jax.ShapeDtypeStruct(x.shape, F32),
            jax.ShapeDtypeStruct(o.shape, BF16),
            jax.ShapeDtypeStruct((width, model_width, TILE), BF16),
            jax.ShapeDtypeStruct((1, model_width), F32),
        ),
        in_specs=[
            row_spec,
            full_spec(o.shape),
            row_spec,
            full_spec(gain.shape),
            pl.BlockSpec((width, model_width, TILE), lambda c: (0, 0, 2)),
            w_spec,
        ],
        out_specs=(
            w_spec,
            row_spec,
            row_spec,
            full_spec(o.shape),
            full_spec((width, model_width, TILE)),
            full_spec((1, model_width)),
        ),
        scratch_shapes=[
            pltpu.VMEM((own_rows, 1024), BF16),
            pltpu.VMEM((own_rows, 1024), F32),
            pltpu.VMEM((own_rows, model_width), BF16),
            pltpu.VMEM((model_width, own_rows), BF16),
            pltpu.VMEM((model_width, own_rows), BF16),
            rows_f32,
            pltpu.VMEM((own_rows, 1), F32),
            rows_f32,
            rows_f32,
            pltpu.VMEM((own_rows, block), BF16),
            pltpu.VMEM((own_rows, block), BF16),
            pltpu.VMEM((own_rows, block), BF16),
        ],
        compiler_params=pltpu.CompilerParams(vmem_limit_bytes=VMEM_BYTES),
        name="middle",
    )(x, o, cot, gain, w_a, w_b)


def finish_kernel(
    x_ref, gain_ref, w_ref, cos_ref, sin_ref, dq_ref, dkv_ref, rg_ref, g_ref, out_ref, gain_grad_ref, wide_scr
):
    own_rows, model_width = x_ref.shape
    width = w_ref.shape[0]
    half_rows = own_rows // 2
    block = (QUERY_FEATURES + 2 * KEY_FEATURES) // width

    def low_piece(i):
        if i < QUERY_HEADS:
            g, j = divmod(i, HEADS_PER_GROUP)
            rows = slice(j * half_rows, (j + 1) * half_rows)
            whole = jnp.concatenate([dq_ref[g, 0, rows, :], dq_ref[g, 1, rows, :]], axis=0)
            return keep_low(whole * 0.125)
        g = (i - QUERY_HEADS) % KEY_VALUE_HEADS
        whole = (
            dkv_ref[g, 0].astype(F32) + dkv_ref[g, 1].astype(F32) + dkv_ref[g, 2].astype(F32)
        )
        if i < QUERY_HEADS + KEY_VALUE_HEADS:
            return keep_low(whole)
        return keep_low(swap_halves(whole))

    for p in range(13):
        chunk = low_piece(2 * p)
        if 2 * p + 1 < QUERY_HEADS + 2 * KEY_VALUE_HEADS:
            chunk = chunk + swap_halves(low_piece(2 * p + 1))
        if p < 10:
            chunk = turn(chunk, cos_ref[...], -sin_ref[...])
        wide_scr[:, p * LANES : (p + 1) * LANES] = chunk.astype(BF16)
    inputs_f = x_ref[...].astype(F32)
    scale = rms_scale(inputs_f)
    normed = inputs_f * scale
    xn_t = (normed * gain_ref[...]).astype(BF16).T
    xg = jnp.zeros((own_rows, model_width), F32)
    for c in range(width):
        part = wide_scr[:, c * block : (c + 1) * block]
        xg = xg + nt(part, w_ref[c, :, :block])
        g_ref[c, :, :block] = nn(xn_t, part).astype(BF16)
        g_ref[c, :, block:] = jnp.zeros((model_width, g_ref.shape[2] - block), BF16)
    gain_grad_ref[...] = jnp.sum(xg * normed, axis=0, keepdims=True)
    e = xg * gain_ref[...]
    out_ref[...] = (
        rg_ref[...] + scale * (e - normed * jnp.mean(e * normed, axis=1, keepdims=True))
    ).astype(BF16)


def finish(x, gain, w_a, cosine, sine, dq, dkv, rg):
    own_rows, model_width = x.shape
    width = w_a.shape[0]
    w_spec = pl.BlockSpec((width, model_width, 512), lambda i: (0, 0, 0))
    return pl.pallas_call(
        finish_kernel,
        grid=(1,),
        out_shape=(
            jax.ShapeDtypeStruct((width, model_width, 512), BF16),
            jax.ShapeDtypeStruct(x.shape, BF16),
            jax.ShapeDtypeStruct((1, model_width), F32),
        ),
        in_specs=[
            full_spec(x.shape),
            full_spec(gain.shape),
            w_spec,
            full_spec(cosine.shape),
            full_spec(sine.shape),
            full_spec(dq.shape),
            full_spec(dkv.shape),
            full_spec(rg.shape),
        ],
        out_specs=(
            w_spec,
            full_spec(x.shape),
            full_spec((1, model_width)),
        ),
        scratch_shapes=[pltpu.VMEM((own_rows, 13 * LANES), BF16)],
        compiler_params=pltpu.CompilerParams(vmem_limit_bytes=VMEM_BYTES),
        name="finish",
    )(x, gain, w_a, cosine, sine, dq, dkv, rg)


def rotation_tables(position):
    half = HEAD_DIMENSION // 2
    lanes = jnp.arange(LANES, dtype=jnp.int32)
    inverse = jnp.exp((lanes % half).astype(F32) * (-2.0 * math.log(THETA) / HEAD_DIMENSION))
    sign = jnp.where(lanes % HEAD_DIMENSION < half, -1.0, 1.0)
    angles = position.astype(F32)[:, None] * inverse[None, :]
    return jnp.cos(angles), jnp.sin(angles) * sign[None, :]


MESH = pl.DeviceIdType.MESH
ANY_SPEC = pl.BlockSpec(memory_space=pl.ANY)


def remote(src, dst, send_sem, recv_sem, device):
    return pltpu.make_async_remote_copy(
        src_ref=src,
        dst_ref=dst,
        send_sem=send_sem,
        recv_sem=recv_sem,
        device_id=device,
        device_id_type=MESH,
    )


def loop(count, body):
    def step(i, carry):
        body(i)
        return carry

    lax.fori_loop(0, count, step, 0)


def signal(device):
    pl.semaphore_signal(
        pltpu.get_barrier_semaphore(), inc=1, device_id=device, device_id_type=MESH
    )


class Place:
    def __init__(self, n_row, n_col):
        self.n_row, self.n_col, self.n_z = n_row, n_col, n_row // 2
        self.row, self.col = lax.axis_index("row"), lax.axis_index("col")
        self.z, self.x = self.row // 2, lax.rem(self.row, 2)
        self.y, self.k = self.col // 2, lax.rem(self.col, 2)
        self.second = self.x + self.k * (self.y - self.x)
        self.third = self.y + self.k * (self.x - self.y)
        self.partner = (self.row, 2 * self.y + (1 - self.k))
        self.by_second = self.device(self.z, 1 - self.second, self.third)
        self.by_third = self.device(self.z, self.second, 1 - self.third)

    def xy(self, second, third):
        return second + self.k * (third - second), third + self.k * (second - third)

    def device(self, z, second, third):
        x, y = self.xy(second, third)
        return (2 * z + x, 2 * y + self.k)

    def along_z(self, z):
        return (2 * z + self.x, self.col)

    def greet(self, with_cols):
        row, col, n_row, n_col = self.row, self.col, self.n_row, self.n_col
        loop(n_row - 1, lambda i: signal((lax.rem(row + 1 + i, n_row), col)))
        if with_cols:
            loop(n_col - 1, lambda i: signal((row, lax.rem(col + 1 + i, n_col))))
            count = n_col - 1
        else:
            signal(self.partner)
            signal((row, lax.rem(col + 2, 4)))
            count = 2
        pl.semaphore_wait(pltpu.get_barrier_semaphore(), n_row - 1 + count)


def slot(ref, kind, col, row, rows):
    if len(ref.shape) == 5:
        return ref.at[col, kind, row]
    return ref.at[col, kind, pl.ds(pl.multiple_of(row * rows, 8), rows), :]


def spread_shape(n_row, n_col, kinds, rows, columns):
    if rows % 8:
        return (n_col, kinds, n_row, rows, columns)
    return (n_col, kinds, n_row * rows, columns)


def deal_copies(me, src, dst, send_sems, recv_sems, i):
    block = src.shape[0] // me.n_row
    peer = lax.rem(me.row + 1 + i, me.n_row)
    giver = lax.rem(me.row + 2 * me.n_row - 1 - i, me.n_row)

    def rows(r):
        return pl.ds(pl.multiple_of(r * block, 8), block)

    out = remote(
        src.at[rows(peer), :], dst.at[rows(me.row), :], send_sems.at[i], recv_sems.at[i], (peer, me.col)
    )
    arrival = remote(
        src.at[rows(peer), :], dst.at[rows(giver), :], send_sems.at[i], recv_sems.at[i], (peer, me.col)
    )
    return out, arrival


def own_block(me, src, dst, sem):
    block = src.shape[0] // me.n_row
    rows = pl.ds(pl.multiple_of(me.row * block, 8), block)
    return pltpu.make_async_copy(src.at[rows, :], dst.at[rows, :], sem)


def gather_kernel(
    n_row,
    n_col,
    x_in,
    cot_in,
    a_in,
    b_in,
    x_out,
    cot_out,
    a_out,
    b_out,
    local_sems,
    deal_send,
    deal_recv,
    z_send,
    z_recv,
    own_send,
    s2_send,
    s2_recv,
    s3_send,
    s3_recv,
    p_send,
    p_recv,
):
    me = Place(n_row, n_col)
    n_z = me.n_z
    rows = a_in.shape[1]
    chunks = [(a_in, a_out, 0)] + [(b_in, b_out, kind) for kind in range(b_in.shape[0])]
    count = len(chunks)

    def at(q, z, second, third, k):
        _, dst, kind = chunks[q]
        x, y = me.xy(second, third)
        return slot(dst, kind, 2 * y + k, 2 * z + x, rows)

    def own(q):
        src, _, kind = chunks[q]
        return src.at[kind]

    def to_z(q, i):
        peer = lax.rem(me.z + 1 + i, n_z)
        return remote(
            own(q), at(q, me.z, me.second, me.third, me.k), z_send.at[q, i], z_recv.at[q, i], me.along_z(peer)
        )

    def from_z(q, i):
        giver = lax.rem(me.z + 2 * n_z - 1 - i, n_z)
        return giver, remote(
            own(q), at(q, giver, me.second, me.third, me.k), z_send.at[q, i], z_recv.at[q, i], me.along_z(giver)
        )

    def to_second(q, z, src):
        return remote(
            src, at(q, z, me.second, me.third, me.k), s2_send.at[q, z], s2_recv.at[q, z], me.by_second
        )

    def to_third(q, z, second, src):
        return remote(
            src, at(q, z, second, me.third, me.k), s3_send.at[q, second, z], s3_recv.at[q, second, z], me.by_third
        )

    def to_partner(q, z, second, third, src):
        x, y = me.xy(second, third)
        index = 2 * x + y
        return remote(
            src, at(q, z, second, third, me.k), p_send.at[q, index, z], p_recv.at[q, index, z], me.partner
        )

    me.greet(False)
    locals_ = [own_block(me, x_in, x_out, local_sems.at[0]), own_block(me, cot_in, cot_out, local_sems.at[1])]
    for q in range(count):
        locals_.append(
            pltpu.make_async_copy(own(q), at(q, me.z, me.second, me.third, me.k), local_sems.at[2 + q])
        )
    for copy in locals_:
        copy.start()

    def begin(q):
        loop(n_z - 1, lambda i: to_z(q, i).start())
        to_second(q, me.z, own(q)).start()
        to_third(q, me.z, me.second, own(q)).start()
        to_partner(q, me.z, me.second, me.third, own(q)).start()

    def deal(src, dst, index):
        loop(n_row - 1, lambda i: deal_copies(me, src, dst, deal_send.at[index], deal_recv.at[index], i)[0].start())

    deal(x_in, x_out, 0)
    for q in range(count):
        begin(q)
    deal(cot_in, cot_out, 1)

    def pass_z(q):
        def one(i):
            giver, arrival = from_z(q, i)
            arrival.wait_recv()
            src = at(q, giver, me.second, me.third, me.k)
            to_second(q, giver, src).start()
            to_third(q, giver, me.second, src).start()
            to_partner(q, giver, me.second, me.third, src).start()

        loop(n_z - 1, one)

    def pass_second(q):
        def one(z):
            src = at(q, z, 1 - me.second, me.third, me.k)
            remote(src, src, s2_send.at[q, z], s2_recv.at[q, z], me.by_second).wait_recv()
            to_third(q, z, 1 - me.second, src).start()
            to_partner(q, z, 1 - me.second, me.third, src).start()

        loop(n_z, one)

    def pass_third(q):
        def one(i):
            second, z = i // n_z, lax.rem(i, n_z)
            src = at(q, z, second, 1 - me.third, me.k)
            remote(
                src, src, s3_send.at[q, second, z], s3_recv.at[q, second, z], me.by_third
            ).wait_recv()
            to_partner(q, z, second, 1 - me.third, src).start()

        loop(2 * n_z, one)

    for t in range(count + 2):
        if t < count:
            pass_z(t)
        if 0 <= t - 1 < count:
            pass_second(t - 1)
        if 0 <= t - 2 < count:
            pass_third(t - 2)

    for q in range(count):

        def from_partner(i, q=q):
            index, z = i // n_z, lax.rem(i, n_z)
            _, dst, kind = chunks[q]
            src = slot(dst, kind, 2 * lax.rem(index, 2) + 1 - me.k, 2 * z + index // 2, rows)
            copy = remote(src, src, p_send.at[q, index, z], p_recv.at[q, index, z], me.partner)
            copy.wait_recv()
            copy.wait_send()

        loop(4 * n_z, from_partner)
        loop(n_z - 1, lambda i, q=q: to_z(q, i).wait_send())
        loop(n_z, lambda z, q=q: to_second(q, z, own(q)).wait_send())
        loop(2 * n_z, lambda i, q=q: to_third(q, lax.rem(i, n_z), i // n_z, own(q)).wait_send())
    for index, (src, dst) in enumerate(((x_in, x_out), (cot_in, cot_out))):

        def finish_deal(i, index=index, src=src, dst=dst):
            out, arrival = deal_copies(me, src, dst, deal_send.at[index], deal_recv.at[index], i)
            out.wait_send()
            arrival.wait_recv()

        loop(n_row - 1, finish_deal)
    for copy in locals_:
        copy.wait()


def gather_all(n_row, n_col, x, cot, pack_a, pack_b):
    n_z = n_row // 2
    rows = pack_a.shape[1]
    count = 1 + pack_b.shape[0]
    dma = pltpu.SemaphoreType.DMA
    a_shape = spread_shape(n_row, n_col, 1, rows, pack_a.shape[2])
    b_shape = spread_shape(n_row, n_col, pack_b.shape[0], rows, pack_b.shape[2])
    x, cot, w_a, w_b = pl.pallas_call(
        functools.partial(gather_kernel, n_row, n_col),
        out_shape=(
            jax.ShapeDtypeStruct(x.shape, BF16),
            jax.ShapeDtypeStruct(cot.shape, BF16),
            jax.ShapeDtypeStruct(a_shape, BF16),
            jax.ShapeDtypeStruct(b_shape, BF16),
        ),
        in_specs=[ANY_SPEC] * 4,
        out_specs=(ANY_SPEC,) * 4,
        scratch_shapes=[
            dma((2 + count,)),
            dma((2, n_row - 1)),
            dma((2, n_row - 1)),
            dma((count, n_z)),
            dma((count, n_z)),
            dma((count,)),
            dma((count, n_z)),
            dma((count, n_z)),
            dma((count, 2, n_z)),
            dma((count, 2, n_z)),
            dma((count, 4, n_z)),
            dma((count, 4, n_z)),
        ],
        compiler_params=pltpu.CompilerParams(collective_id=0, has_side_effects=True),
        name="gather_all",
    )(x, cot, pack_a, pack_b)
    model_width = n_row * rows
    w_a = w_a.reshape(n_col, model_width, pack_a.shape[2])
    w_b = w_b.reshape(n_col, pack_b.shape[0], model_width, pack_b.shape[2])
    return x, cot, w_a, w_b


def window_kernel(kv_in, kv_out, local_sem, send_a, recv_a, send_b, recv_b):
    row, col = lax.axis_index("row"), lax.axis_index("col")
    groups = kv_in.shape[0]

    def far(g, src, device):
        return remote(src, kv_out.at[g, 0], send_a.at[g], recv_a.at[g], device)

    def near(g, src, device):
        return remote(src, kv_out.at[g, 1], send_b.at[g], recv_b.at[g], device)

    for other in range(1, 4):
        signal((row, lax.rem(col + other, 4)))
    pl.semaphore_wait(pltpu.get_barrier_semaphore(), 3)
    local = pltpu.make_async_copy(kv_in, kv_out.at[:, 2], local_sem)
    local.start()

    @pl.when(col < 2)
    def _():
        loop(groups, lambda g: far(g, kv_in.at[g], (row, col + 2)).start())

    @pl.when(lax.rem(col, 2) == 0)
    def _():
        loop(groups, lambda g: near(g, kv_in.at[g], (row, col + 1)).start())

    @pl.when(col == 2)
    def _():
        def one(g):
            far(g, kv_in.at[g], (row, 0)).wait_recv()
            near(g, kv_in.at[g], (row, 3)).wait()

        loop(groups, one)

    @pl.when(col == 3)
    def _():
        def one(g):
            far(g, kv_in.at[g], (row, 1)).wait_recv()
            near(g, kv_out.at[g, 0], (row, 2)).start()

        def two(g):
            near(g, kv_out.at[g, 0], (row, 2)).wait()

        loop(groups, one)
        loop(groups, two)

    @pl.when(col == 1)
    def _():
        loop(groups, lambda g: near(g, kv_in.at[g], (row, 0)).wait_recv())

    @pl.when(col == 0)
    def _():
        loop(groups, lambda g: near(g, kv_in.at[g], (row, 1)).wait_send())

    @pl.when(col < 2)
    def _():
        loop(groups, lambda g: far(g, kv_in.at[g], (row, col + 2)).wait_send())

    local.wait()


def key_window(kv):
    groups, own_rows, lanes = kv.shape
    dma = pltpu.SemaphoreType.DMA
    out = pl.pallas_call(
        window_kernel,
        out_shape=jax.ShapeDtypeStruct((groups, 3, own_rows, lanes), BF16),
        in_specs=[ANY_SPEC],
        out_specs=ANY_SPEC,
        scratch_shapes=[dma, dma((groups,)), dma((groups,)), dma((groups,)), dma((groups,))],
        compiler_params=pltpu.CompilerParams(collective_id=1, has_side_effects=True),
        name="key_window",
    )(kv)
    return out.reshape(groups, 3 * own_rows, lanes)


def return_kernel(dkv_in, dkv_out, mail, local_sem, send_a, recv_a, send_b, recv_b):
    row, col = lax.axis_index("row"), lax.axis_index("col")
    groups = dkv_in.shape[0]

    def far(g, src, device):
        return remote(src, dkv_out.at[g, 2], send_a.at[g], recv_a.at[g], device)

    def near(g, device):
        return remote(dkv_in.at[g, 1], dkv_out.at[g, 1], send_b.at[g], recv_b.at[g], device)

    def aside(g):
        return remote(dkv_in.at[g, 1], mail.at[g], send_b.at[g], recv_b.at[g], (row, 3))

    for other in range(1, 4):
        signal((row, lax.rem(col + other, 4)))
    pl.semaphore_wait(pltpu.get_barrier_semaphore(), 3)
    for g in range(groups):
        dkv_out[g, 0] = dkv_in[g, 2]

    @pl.when(col == 2)
    def _():
        def one(g):
            aside(g).start()
            far(g, dkv_in.at[g, 0], (row, 0)).start()

        loop(groups, one)

    @pl.when(col == 3)
    def _():
        loop(groups, lambda g: near(g, (row, 2)).start())

        def one(g):
            aside(g).wait_recv()
            mail[g] = (mail[g].astype(F32) + dkv_in[g, 0].astype(F32)).astype(BF16)
            far(g, mail.at[g], (row, 1)).start()

        loop(groups, one)

    @pl.when(col == 1)
    def _():
        loop(groups, lambda g: near(g, (row, 0)).start())

    @pl.when(lax.rem(col, 2) == 1)
    def _():
        for g in range(groups):
            dkv_out[g, 1] = jnp.zeros(dkv_out.shape[2:], BF16)

    @pl.when(col >= 2)
    def _():
        for g in range(groups):
            dkv_out[g, 2] = jnp.zeros(dkv_out.shape[2:], BF16)

    @pl.when(col < 2)
    def _():
        loop(groups, lambda g: far(g, mail.at[g], (row, col + 2)).wait_recv())

    @pl.when(col == 0)
    def _():
        loop(groups, lambda g: near(g, (row, 1)).wait_recv())

    @pl.when(col == 1)
    def _():
        loop(groups, lambda g: near(g, (row, 0)).wait_send())

    @pl.when(col == 2)
    def _():
        def one(g):
            near(g, (row, 3)).wait_recv()
            aside(g).wait_send()
            far(g, dkv_in.at[g, 0], (row, 0)).wait_send()

        loop(groups, one)

    @pl.when(col == 3)
    def _():
        def one(g):
            near(g, (row, 2)).wait_send()
            far(g, mail.at[g], (row, 1)).wait_send()

        loop(groups, one)


def return_keys(dkv):
    groups, window, lanes = dkv.shape
    own_rows = window // 3
    dma = pltpu.SemaphoreType.DMA
    vmem = pl.BlockSpec(memory_space=pltpu.VMEM)
    return pl.pallas_call(
        return_kernel,
        out_shape=jax.ShapeDtypeStruct((groups, 3, own_rows, lanes), BF16),
        in_specs=[vmem],
        out_specs=vmem,
        scratch_shapes=[
            pltpu.VMEM((groups, own_rows, lanes), BF16),
            dma,
            dma((groups,)),
            dma((groups,)),
            dma((groups,)),
            dma((groups,)),
        ],
        compiler_params=pltpu.CompilerParams(
            collective_id=2, has_side_effects=True, vmem_limit_bytes=VMEM_BYTES
        ),
        name="return_keys",
    )(dkv.reshape(groups, 3, own_rows, lanes))


class Stage:
    pass


def reduce_kernel(n_row, n_col, rows, layer_in, grad_in, gain_in, *refs):
    me = Place(n_row, n_col)
    n_z = me.n_z
    n_chunk = 5
    parts, refs = refs[:3], refs[3:]
    (layer_out, grad_out, gain_out, o_q, o_o, o_b), refs = refs[:6], refs[6:]
    (
        own_scr,
        ra_scr,
        rb_scr,
        rc_scr,
        rd_scr,
        gain_scr,
        gain_sum,
    ), refs = refs[:7], refs[7:]
    (
        local_sems,
        deal_send,
        deal_recv,
        col_send,
        col_recv,
        row_send,
        row_recv,
        load_sems,
        a_send,
        a_recv,
        b_send,
        b_recv,
        c_send,
        c_recv,
        d_send,
        d_recv,
    ) = refs
    g_q, g_o, g_b = parts
    chunks = [
        (g_b, 2, 640, lambda v: o_b.__setitem__(2, v)),
        (g_b, 0, 640, lambda v: o_b.__setitem__(0, v)),
        (g_b, 1, 640, lambda v: o_b.__setitem__(1, v)),
        (g_o, 0, 256, lambda v: o_o.__setitem__(0, v)),
        (g_q, 0, 512, lambda v: o_q.__setitem__(0, v)),
    ]

    def view(scr, q, *index):
        return scr.at[(q, *index, slice(None), pl.ds(0, chunks[q][2]))]

    def index_of(second, third):
        x, y = me.xy(second, third)
        return 2 * x + y

    def grad_at(q, xy, z, k):
        ref, kind, _, _ = chunks[q]
        return slot(ref, kind, 2 * lax.rem(xy, 2) + k, 2 * z + xy // 2, rows)

    def load(q, xy, z):
        return pltpu.make_async_copy(
            grad_at(q, xy, z, me.k), view(own_scr, q, xy, z), load_sems.at[q, xy, z]
        )

    def give(q, xy, z):
        return remote(
            grad_at(q, xy, z, 1 - me.k),
            view(ra_scr, q, xy, z),
            a_send.at[q, xy, z],
            a_recv.at[q, xy, z],
            me.partner,
        )

    def to_third(q, second, z):
        return remote(
            view(own_scr, q, index_of(second, 1 - me.third), z),
            view(rb_scr, q, second, z),
            b_send.at[q, second, z],
            b_recv.at[q, second, z],
            me.by_third,
        )

    def to_second(q, z):
        return remote(
            view(own_scr, q, index_of(1 - me.second, me.third), z),
            view(rc_scr, q, z),
            c_send.at[q, z],
            c_recv.at[q, z],
            me.by_second,
        )

    def to_z(q, i):
        peer = lax.rem(me.z + 1 + i, n_z)
        return remote(
            view(own_scr, q, index_of(me.second, me.third), peer),
            view(rd_scr, q, i),
            d_send.at[q, i],
            d_recv.at[q, i],
            me.along_z(peer),
        )

    def add(q, xy, z, other):
        mine = view(own_scr, q, xy, z)
        mine[...] = (mine[...].astype(F32) + other[...].astype(F32)).astype(BF16)

    def take_partner(q, xy, z):
        load(q, xy, z).wait()
        give(q, xy, z).wait_recv()
        add(q, xy, z, view(ra_scr, q, xy, z))

    def stage_b(q):
        def send(i):
            second = (1 - me.second) + (i // n_z) * (2 * me.second - 1)
            z = lax.rem(i, n_z)
            take_partner(q, index_of(second, 1 - me.third), z)
            to_third(q, second, z).start()

        loop(2 * n_z, send)

        def keep(i):
            second = (1 - me.second) + (i // n_z) * (2 * me.second - 1)
            take_partner(q, index_of(second, me.third), lax.rem(i, n_z))

        loop(2 * n_z, keep)

    def stage_c(q):
        def one(i):
            second = (1 - me.second) + (i // n_z) * (2 * me.second - 1)
            z = lax.rem(i, n_z)
            to_third(q, second, z).wait_recv()
            add(q, index_of(second, me.third), z, view(rb_scr, q, second, z))

        loop(n_z, lambda z: (one(z), to_second(q, z).start()))
        loop(n_z, lambda z: one(z + n_z))

    def stage_d(q):
        mine = index_of(me.second, me.third)

        def one(i):
            peer = lax.rem(me.z + 1 + i, n_z)
            to_second(q, peer).wait_recv()
            add(q, mine, peer, view(rc_scr, q, peer))

        loop(n_z - 1, lambda i: (one(i), to_z(q, i).start()))
        one(n_z - 1)

    def stage_e(q):
        mine = view(own_scr, q, index_of(me.second, me.third), me.z)
        loop(n_z - 1, lambda i: to_z(q, i).wait_recv())
        total = mine[...].astype(F32)
        for i in range(n_z - 1):
            total = total + view(rd_scr, q, i)[...].astype(F32)
        chunks[q][3](total)

    me.greet(True)
    locals_ = [
        own_block(me, layer_in, layer_out, local_sems.at[0]),
        own_block(me, grad_in, grad_out, local_sems.at[1]),
    ]
    for copy in locals_:
        copy.start()

    def col_copy(i):
        peer = lax.rem(me.col + 1 + i, n_col)
        return remote(
            gain_in, gain_scr.at[me.col], col_send.at[i], col_recv.at[i], (me.row, peer)
        )

    def row_copy(i):
        peer = lax.rem(me.row + 1 + i, n_row)
        return remote(
            gain_sum, gain_scr.at[n_col + me.row], row_send.at[i], row_recv.at[i], (peer, me.col)
        )

    loop(n_col - 1, lambda i: col_copy(i).start())
    for q in range(n_chunk):

        def begin(i, q=q):
            second = (1 - me.second) + lax.rem(i // n_z, 2) * (2 * me.second - 1)
            third = (1 - me.third) + (i // (2 * n_z)) * (2 * me.third - 1)
            z = lax.rem(i, n_z)
            load(q, index_of(second, third), z).start()
            give(q, i // n_z, z).start()

        loop(4 * n_z, begin)
    for index, (src, dst) in enumerate(((layer_in, layer_out), (grad_in, grad_out))):
        loop(
            n_row - 1,
            lambda i, src=src, dst=dst, index=index: deal_copies(
                me, src, dst, deal_send.at[index], deal_recv.at[index], i
            )[0].start(),
        )
    gain_scr[me.col] = gain_in[...]
    loop(n_col - 1, lambda i: col_copy(i).wait_recv())
    total = gain_scr[0]
    for c in range(1, n_col):
        total = total + gain_scr[c]
    gain_sum[...] = total
    gain_scr[n_col + me.row] = total
    loop(n_row - 1, lambda i: row_copy(i).start())

    for t in range(n_chunk + 3):
        if t < n_chunk:
            stage_b(t)
        if 0 <= t - 1 < n_chunk:
            stage_c(t - 1)
        if 0 <= t - 2 < n_chunk:
            stage_d(t - 2)
        if 0 <= t - 3 < n_chunk:
            stage_e(t - 3)

    loop(n_row - 1, lambda i: row_copy(i).wait_recv())
    total = gain_scr[n_col]
    for r in range(1, n_row):
        total = total + gain_scr[n_col + r]
    gain_out[...] = total

    loop(n_col - 1, lambda i: col_copy(i).wait_send())
    loop(n_row - 1, lambda i: row_copy(i).wait_send())
    for q in range(n_chunk):
        loop(4 * n_z, lambda i, q=q: give(q, i // n_z, lax.rem(i, n_z)).wait_send())
        loop(2 * n_z, lambda i, q=q: to_third(q, i // n_z, lax.rem(i, n_z)).wait_send())
        loop(n_z, lambda z, q=q: to_second(q, z).wait_send())
        loop(n_z - 1, lambda i, q=q: to_z(q, i).wait_send())
    for index, (src, dst) in enumerate(((layer_in, layer_out), (grad_in, grad_out))):

        def finish_deal(i, index=index, src=src, dst=dst):
            out, arrival = deal_copies(me, src, dst, deal_send.at[index], deal_recv.at[index], i)
            out.wait_send()
            arrival.wait_recv()

        loop(n_row - 1, finish_deal)
    for copy in locals_:
        copy.wait()


def reduce_all(n_row, n_col, layer_out, grad_in, gains, g_q, g_o, g_b):
    n_z = n_row // 2
    rows = g_b.shape[2] // n_row
    dma = pltpu.SemaphoreType.DMA
    vmem = pl.BlockSpec(memory_space=pltpu.VMEM)
    n_chunk = 5

    def shaped(values, kinds):
        return values.reshape(spread_shape(n_row, n_col, kinds, rows, values.shape[-1]))

    return pl.pallas_call(
        functools.partial(reduce_kernel, n_row, n_col, rows),
        out_shape=(
            jax.ShapeDtypeStruct(layer_out.shape, BF16),
            jax.ShapeDtypeStruct(grad_in.shape, BF16),
            jax.ShapeDtypeStruct(gains.shape, F32),
            jax.ShapeDtypeStruct((1, rows, g_q.shape[-1]), F32),
            jax.ShapeDtypeStruct((1, rows, g_o.shape[-1]), F32),
            jax.ShapeDtypeStruct((3, rows, g_b.shape[-1]), F32),
        ),
        in_specs=[ANY_SPEC, ANY_SPEC, vmem, ANY_SPEC, ANY_SPEC, ANY_SPEC],
        out_specs=(ANY_SPEC, ANY_SPEC, vmem, vmem, vmem, vmem),
        scratch_shapes=[
            pltpu.VMEM((n_chunk, 4, n_z, rows, 640), BF16),
            pltpu.VMEM((n_chunk, 4, n_z, rows, 640), BF16),
            pltpu.VMEM((n_chunk, 2, n_z, rows, 640), BF16),
            pltpu.VMEM((n_chunk, n_z, rows, 640), BF16),
            pltpu.VMEM((n_chunk, n_z - 1, rows, 640), BF16),
            pltpu.VMEM((n_col + n_row, *gains.shape), F32),
            pltpu.VMEM(gains.shape, F32),
            dma((2,)),
            dma((2, n_row - 1)),
            dma((2, n_row - 1)),
            dma((n_col - 1,)),
            dma((n_col - 1,)),
            dma((n_row - 1,)),
            dma((n_row - 1,)),
            dma((n_chunk, 4, n_z)),
            dma((n_chunk, 4, n_z)),
            dma((n_chunk, 4, n_z)),
            dma((n_chunk, 2, n_z)),
            dma((n_chunk, 2, n_z)),
            dma((n_chunk, n_z)),
            dma((n_chunk, n_z)),
            dma((n_chunk, n_z)),
            dma((n_chunk, n_z)),
        ],
        compiler_params=pltpu.CompilerParams(
            collective_id=3, has_side_effects=True, vmem_limit_bytes=VMEM_BYTES
        ),
        name="reduce_all",
    )(layer_out, grad_in, gains, shaped(g_q, 1), shaped(g_o, 1), shaped(g_b, 3))


def on_device(
    layer_input,
    norm1_gain,
    w_qkv,
    w_out,
    norm2_gain,
    w_gate,
    w_up,
    w_down,
    out_cotangent,
    seq_lengths,
    position_ids,
    deal_rows,
):
    own_rows, model_width = layer_input.shape
    n_row = lax.axis_size("row")
    n_col = lax.axis_size("col")
    block_rows = own_rows // n_row
    row_ids = jnp.arange(n_row, dtype=jnp.int32)
    targets = deal_rows[0]
    sender = jnp.sum(jnp.where(targets[:, None] == row_ids[None, :], row_ids[:, None], 0), axis=0)

    def pick(values, order):
        blocks = values.reshape(n_row, block_rows, model_width)
        return jnp.take(blocks, order, axis=0).reshape(own_rows, model_width)

    def pad(values, columns):
        return jnp.pad(values, ((0, 0), (0, columns - values.shape[1])))

    pack_a = jnp.concatenate([pad(w_qkv, 512), pad(w_out, 256)], axis=1)[None]
    pack_b = jnp.stack([w_gate, w_up, w_down])
    x, cot, w_a, w_b = gather_all(
        n_row, n_col, pick(layer_input, sender), pick(out_cotangent, sender), pack_a, pack_b
    )

    gain_one, gain_two = norm1_gain[None, :], norm2_gain[None, :]
    cosine, sine = rotation_tables(position_ids)
    col = lax.axis_index("col")
    bounds = jnp.cumsum(seq_lengths[0])
    own_ids = col * own_rows + jnp.arange(own_rows, dtype=jnp.int32)
    start = jnp.sum(
        jnp.where(own_ids[:, None] >= bounds[None, :], seq_lengths[0][None, :], 0), axis=1
    )
    start = start - (col * own_rows - LONGEST)
    low = jnp.stack([start[0], start[own_rows // 2]]) // TILE
    start = jnp.broadcast_to(start[:, None], (own_rows, LANES)).astype(jnp.int32)

    q, kv_own = project(x, gain_one, w_a, cosine, sine)
    kv = key_window(kv_own)
    o, logsum = attend(low, start, q, kv)
    g_b, layer_out, rg, do, g_o, gain_two_part = middle(x, o, cot, gain_two, w_a, w_b)
    dq, dkv = attend_back(low, start, q, kv, o, do, logsum)
    dkv = return_keys(dkv)
    g_q, grad_in, gain_one_part = finish(x, gain_one, w_a, cosine, sine, dq, dkv, rg)
    gains = jnp.concatenate([gain_one_part, gain_two_part], axis=0)
    gains = jnp.pad(gains, ((0, 6), (0, 1024 - model_width)))
    back_out, back_grad, gains, o_q, o_o, o_b = reduce_all(
        n_row, n_col, layer_out, grad_in, gains, g_q, g_o, g_b
    )
    return (
        pick(back_out, targets),
        pick(back_grad, targets),
        gains[0, :model_width],
        o_q[0, :, : w_qkv.shape[1]],
        o_o[0, :, : w_out.shape[1]],
        gains[1, :model_width],
        o_b[0],
        o_b[1],
        o_b[2],
    )


def solution(mesh):
    placed = (
        P(("row", "col"), None),
        P(),
        P("row", "col"),
        P("row", "col"),
        P(),
        P("row", "col"),
        P("row", "col"),
        P("row", "col"),
        P(("row", "col"), None),
        P("row", None),
        P(("row", "col")),
        P(("row", "col"), None),
    )
    return jax.shard_map(
        on_device,
        mesh=mesh,
        in_specs=placed,
        out_specs=(
            P(("row", "col"), None),
            P(("row", "col"), None),
            P(),
            P("row", "col"),
            P("row", "col"),
            P(),
            P("row", "col"),
            P("row", "col"),
            P("row", "col"),
        ),
        check_vma=False,
    )
```

time: 1590 us -> 478 us (0.30)
  waiting for transfers between devices: 807 us -> 0 us
  Pallas kernels: 0 us -> 450 us
  matrix products: 335 us -> 0 us
  blocking collectives: 178 us -> 0 us
  local copies, waits for them, and re-layouts: 105 us -> 15.7 us
  loops' own time: 59.7 us -> 0 us
  other arithmetic: 47.7 us -> 10.5 us
  starting transfers between devices: 24.6 us -> 0 us
  between operations: 17 us -> 0.91 us
    pallas_call x0 -> x9, Pallas kernels: none -> 450 us  [the longest x1 143 us: reduce_all(): pl.pallas_call(functools.partial(reduce_kernel, n_row, n_col, rows), out_...]
    reduce_scatter x7 -> x0, waiting for transfers between devices: 357 us -> none  [the longest x4 240 us: spread_sum(): return lax.psum_scatter(result, 'col', scatter_dimension=0, tiled=True)]
    dot_general x119 -> x0, matrix products: 328 us -> none  [the longest x50 134 us: matmul_nt(): lax.dot_general(left_mat, right_mat, (((1,), (1,)), ((), ())), preferred_...]
    unnamed x24 -> x0, waiting for transfers between devices: 205 us -> none
    all_gather x9 -> x0, waiting for transfers between devices: 174 us -> none  [the longest x4 77.5 us: gather_rows(): return lax.all_gather(values, 'col', axis=0, tiled=True)]
    all_to_all x3 -> x0, blocking collectives: 84.5 us -> none  [the longest x1 31.2 us: on_device(): lax.all_to_all(input_blocks, 'row', split_axis=0, concat_axis=0, tiled=True)]
    all_to_all x5 -> x0, waiting for transfers between devices: 70.4 us -> none  [the longest x1 37.8 us: on_device(): lax.all_to_all(input_grad.astype(jnp.bfloat16), 'row', split_axis=0, conc...]
    another operation x2 -> x0, loops' own time: 59.7 us -> none  [the longest x1 30.1 us: attend_back(): lax.scan(one_head, (empty, empty), (query_heads, grad_heads, logsum, head...]
  transfers between devices with their start and end apart: 25 -> 0, of which waited for: 22 -> 0; matrix products, arithmetic and copies ran while one was open for 6% -> 0% of each run, Pallas kernels for 0% -> 0%
where the time goes in v1:
time: 478 us; the launch traced here: 477 us
  Pallas kernels  450 us (94%)
  local copies, waits for them, and re-layouts  15.7 us (3%)
  other arithmetic  10.5 us (2%)
    pallas_call x1, Pallas kernels, reduce_all(): pl.pallas_call(functools.partial(reduce_kernel, n_row, n_col, rows), out_...  143 us
    pallas_call x1, Pallas kernels, gather_all(): pl.pallas_call(functools.partial(gather_kernel, n_row, n_col), out_shape=...  141 us
    pallas_call x1, Pallas kernels, middle(): pl.pallas_call(middle_kernel, grid=(width,), out_shape=(jax.ShapeDtypeStr...  48 us
    pallas_call x1, Pallas kernels, return_keys(): pl.pallas_call(return_kernel, out_shape=jax.ShapeDtypeStruct((groups, 3,...  30.9 us
    pallas_call x1, Pallas kernels, key_window(): pl.pallas_call(window_kernel, out_shape=jax.ShapeDtypeStruct((groups, 3,...  24.4 us
    pallas_call x1, Pallas kernels, attend_back(): pl.pallas_call(attend_back_kernel, grid=(groups,), out_shape=(jax.ShapeDt...  23.5 us
    pallas_call x1, Pallas kernels, attend(): pl.pallas_call(attend_kernel, grid=(groups,), out_shape=(jax.ShapeDtypeSt...  19.3 us
    pallas_call x1, Pallas kernels, finish(): pl.pallas_call(finish_kernel, grid=(1,), out_shape=(jax.ShapeDtypeStruct(...  13.6 us

profile of v1, /device:TPU:1, one launch (start us, length us, event | category | flops | bytes accessed | tf_op | source)
XLA Modules:
  0.0 477.3 jit_solution(14400482685326285581)
XLA Ops:
  0.6 0.7 select_reduce_fusion.1
  1.4 1.5 copy.31
  2.9 0.6 gather_fusion
  3.5 1.5 copy.32
  5.0 0.6 gather_fusion.1
  5.7 1.6 broadcast_select_fusion.2
  7.3 0.8 pad_maximum_fusion.b_in
  8.3 0.7 fusion.4.a_in
  9.0 140.9 %gather_all.1 = (bf16[512,960]{1,0:T(8,128)(2,1)}, bf16[512,960]{1,0:T(8,128)(2,1)}, bf16[4,1,960,768]{3,2,1,0:T(8,128)(2,1)}, bf16[4,3,960,640]{3,2,1,0:T(8,128)(2,1)}) custom-call(bf16[512,960]{1,0:T(8,128)(2,1)} %bitcast.45, bf16[512,960]{1,0:T(8,128)(2,1)} %bitcast.44, bf16[1,120,768]{2,1,0:T(8,128)(2,1)} %fusion.4.a_in, ...), custom_call_target="tpu_custom_call" | custom-call | tf_op jit(solution)/shard_map/gather_all/pallas_call | solution.py:835
  150.0 1.8 fusion.2
  151.8 6.8 %project.1 = (bf16[5,2,768,128]{3,2,1,0:T(8,128)(2,1)}, bf16[5,512,128]{2,1,0:T(8,128)(2,1)}) custom-call(bf16[512,960]{1,0:T(8,128)(2,1)} %get-tuple-element.35.x_ref, f32[1,960]{1,0:T(1,128)} %bitcast.58, bf16[4,960,768]{2,1,0:T(8,128)(2,1)} %bitcast.39, f32[512,128]{1,0:T(8,128)} %get-tuple-element.93.cos_ref, f32[512,128]{1,0:T(8,128)} %get-tuple-element.92.sin_ref), custom_call_target="tpu_custom_call" | custom-call | tf_op jit(solution)/shard_map/project/pallas_call | solution.py:115
  158.6 24.4 %key_window.1 = bf16[5,3,512,128]{3,2,1,0:T(8,128)(2,1)} custom-call(bf16[5,512,128]{2,1,0:T(8,128)(2,1)} %get-tuple-element.38.kv_in), custom_call_target="tpu_custom_call" | custom-call | tf_op jit(solution)/shard_map/key_window/pallas_call | solution.py:930
  183.0 0.2 reduce-window.8
  183.2 0.5 fusion.9
  183.8 1.9 and_select_fusion.2.low_ref
  185.7 0.8 broadcast_in_dim.71.start_ref
  186.5 19.3 %attend.1 = (bf16[5,2,768,128]{3,2,1,0:T(8,128)(2,1)}, f32[5,2,768,128]{3,2,1,0:T(8,128)}) custom-call(s32[2]{0:T(128)} %and_select_fusion.2.low_ref, s32[512,128]{1,0:T(8,128)} %broadcast_in_dim.71.start_ref, bf16[5,2,768,128]{3,2,1,0:T(8,128)(2,1)} %get-tuple-element.37.q_ref, bf16[5,1536,128]{2,1,0:T(8,128)(2,1)} %bitcast.42), custom_call_target="tpu_custom_call" | custom-call | tf_op jit(solution)/shard_map/attend/pallas_call | solution.py:203
  205.8 48.0 %middle.1 = (bf16[4,3,960,640]{3,2,1,0:T(8,128)(2,1)}, bf16[512,960]{1,0:T(8,128)(2,1)}, f32[512,960]{1,0:T(8,128)}, bf16[5,2,768,128]{3,2,1,0:T(8,128)(2,1)}, b...) custom-call(bf16[512,960]{1,0:T(8,128)(2,1)} %get-tuple-element.35.x_ref, ...), custom_call_target="tpu_custom_call" | custom-call | tf_op jit(solution)/shard_map/middle/pallas_call | solution.py:439
  253.8 23.5 %attend_back.1 = (f32[5,2,768,128]{3,2,1,0:T(8,128)}, bf16[5,1536,128]{2,1,0:T(8,128)(2,1)}) custom-call(s32[2]{0:T(128)} %and_select_fusion.2.low_ref, s32[512,128]{1,0:T(8,128)} %broadcast_in_dim.71.start_ref, bf16[5,2,768,128]{3,2,1,0:T(8,128)(2,1)} %get-tuple-element.37.q_ref, bf16[5,1536,128]{2,1,0:T(8,128)(2,1)} %bitcast.43, ...), custom_call_target="tpu_custom_call" | custom-call | tf_op jit(solution)/shard_map/attend_back/pallas_call | solution.py:277
  277.3 30.9 %return_keys.1.dkv_ref = bf16[5,3,512,128]{3,2,1,0:T(8,128)(2,1)} custom-call(bf16[5,3,512,128]{3,2,1,0:T(8,128)(2,1)} %bitcast.51), custom_call_target="tpu_custom_call" | custom-call | tf_op jit(solution)/shard_map/return_keys/pallas_call | solution.py:1029
  308.2 13.6 %finish.1 = (bf16[4,960,512]{2,1,0:T(8,128)(2,1)}, bf16[512,960]{1,0:T(8,128)(2,1)}, f32[1,960]{1,0:T(1,128)}) custom-call(bf16[512,960]{1,0:T(8,128)(2,1)} %get-tuple-element.35.x_ref, f32[1,960]{1,0:T(1,128)} %bitcast.59, bf16[4,960,768]{2,1,0:T(8,128)(2,1)} %bitcast.41, f32[512,128]{1,0:T(8,128)} %get-tuple-element.93.cos_ref, ...), custom_call_target="tpu_custom_call" | custom-call | tf_op jit(solution)/shard_map/finish/pallas_call | solution.py:535
  321.8 1.3 select_maximum_fusion.gain_in
  323.1 142.8 %reduce_all.1 = (bf16[512,960]{1,0:T(8,128)(2,1)}, bf16[512,960]{1,0:T(8,128)(2,1)}, f32[8,1024]{1,0:T(8,128)}, f32[1,120,512]{2,1,0:T(8,128)}, f32[1,120,256]{2,1,0:T(8,128)}, /*index=5*/f32[3,120,640]{2,1,0:T(8,128)}) custom-call(bf16[512,960]{1,0:T(8,128)(2,1)} %get-tuple-element.42.layer_in, bf16[512,960]{1,0:T(8,128)(2,1)} %get-tuple-element.48.grad_in, ...), custom_call_target="tpu_custom_call" | custom-call | tf_op jit(solution)/shard_map/reduce_all/pallas_call | solution.py:1293
  466.0 1.9 gather_fusion.2
  467.9 0.6 gather_fusion.3
  468.6 1.2 broadcast_select_fusion
  469.8 2.3 copy.34
  472.1 1.3 copy.35
  473.4 0.9 slice_bitcast_fusion
  474.4 0.8 copy.36
  475.2 0.7 slice_bitcast_fusion.4
  475.9 1.4 fusion.8
  (39 shorter events, 0.3 us)
Async XLA Ops:
  5.6 1.7 copy-start.3
  5.6 1.6 copy-start.4
  5.6 1.6 copy-start.5
  5.7 2.5 copy-start.7
  5.7 2.6 copy-start.8
  7.3 142.6 %copy-start.10 = (s32[512]{0:T(512)S(1)}, s32[512]{0:T(512)}, u32[]{:S(2)}) copy-start(s32[512]{0:T(512)} %param.24) | copy-start | bytes 6148
  158.6 24.4 %copy-start.11 = (s32[1,3]{1,0:T(1,128)S(1)}, s32[1,3]{1,0:T(1,128)}, u32[]{:S(2)}) copy-start(s32[1,3]{1,0:T(1,128)} %param.23) | copy-start | bytes 40
  308.2 13.6 %copy-start.9 = (f32[1,960]{1,0:T(1,128)S(1)}, f32[1,960]{1,0:T(1,128)}, u32[]{:S(2)}) copy-start(f32[1,960]{1,0:T(1,128)} %get-tuple-element.50) | copy-start | bytes 11524
  323.1 142.9 %copy-start.12 = (s32[1,8]{1,0:T(1,128)S(1)}, s32[1,8]{1,0:T(1,128)}, u32[]{:S(2)}) copy-start(s32[1,8]{1,0:T(1,128)} %param.25) | copy-start | bytes 100
  466.0 2.0 copy-start
  469.8 3.6 copy-start.1
  472.1 2.2 copy-start.2
  472.1 3.1 copy-start.6
